TPU v7x, 32 devices: a whole 2x2x4 slice. The times are simulated.
32 devices in a mesh: cam: 2 (over core), tile: 16 (over z, y, x).
Axes of the slice: x: 2, y: 2, z: 4, core: 2. Of those that a mesh axis runs over, the one named last changes fastest.
Arguments:
- queries: bfloat16 [4096, 256], P('tile'), as said below
- keys: bfloat16 [2048, 256], P(('cam', 'tile')), as said below
- values: bfloat16 [2048, 256], P(('cam', 'tile')), may hold values from -6 to 6
- grad_out: bfloat16 [4096, 256], P('tile'), may hold values from -6 to 6
- visible: int32 [32, 64], P('tile', 'cam'), may hold values from 0 to 1, as said below
- counts: int32 [64], P('cam'), may hold values from 2 to 32
Outputs:
- grad_queries: bfloat16 [4096, 256], P('tile')
- grad_keys: bfloat16 [2048, 256], P(('cam', 'tile'))
- grad_values: bfloat16 [2048, 256], P(('cam', 'tile'))
Inputs may be any that keep to these rules, and one draw needn't show every extreme that they name: Every tile has at least one visible block. `queries`: projected query features. `keys`: projected key features.
All inputs are finite; a program needn't handle non-finite values.
Results may differ from a plain program's by a relative error of at most 0.0052.
Values may be sent and summed in bfloat16 or wider, within the bound.
No kernel may reach another device: no remote copies, remote signals or barrier semaphores. Data moves between devices by JAX's collectives and lax.ppermute only.
A program may use at most 128 MiB of HBM per device.

v0:
```python
import functools
import math

import jax
import jax.numpy as jnp
from jax import lax
from jax.experimental import pallas as pl
from jax.experimental.pallas import tpu as pltpu
from jax.sharding import PartitionSpec as P


H = 8
LANES = 128
FAR = -1e30
BF16 = jnp.bfloat16
F32 = jnp.float32


def dot(a, b, dims):
    return lax.dot_general(a, b, (dims, ((), ())), preferred_element_type=F32)


NN = ((1,), (0,))
NT = ((1,), (1,))


def step_orders(tiles):
    bits = []
    bit = tiles // 4
    while bit >= 1:
        bits.append(bit)
        bit //= 2
    return (tuple(bits), tuple(bits[-1:] + bits[:-1]))


def slot_masks(order):
    masks = [0]
    for bit in order:
        masks = masks + [mask ^ bit for mask in masks]
    return masks


def build_bias(where_ref, table_ref, bias_ref, masks, shard_rows, block_keys):
    tile, cam = where_ref[0], where_ref[1]
    per_shard = shard_rows // block_keys
    lanes = table_ref.shape[1]
    table = table_ref[...]
    lane = lax.broadcasted_iota(jnp.int32, (shard_rows, lanes), 1)
    row = lax.broadcasted_iota(jnp.int32, (shard_rows, lanes), 0)
    place = lax.broadcasted_iota(jnp.int32, (shard_rows, LANES), 0) % block_keys
    column = lax.broadcasted_iota(jnp.int32, (shard_rows, LANES), 1)
    for slot in range(len(masks[0])):
        mask = jnp.where(cam % 2 == 0, masks[0][slot], masks[1][slot])
        block = (tile ^ mask) * per_shard + row // block_keys
        picked = dot((lane == block).astype(F32).astype(BF16), table, NT)
        count = picked[:, LANES - 1 : LANES]
        allowed = (picked > 0.5) & (place.astype(F32) < count)
        bias = jnp.where(allowed | (column == LANES - 1), 0.0, FAR)
        bias_ref[slot * shard_rows : (slot + 1) * shard_rows, :] = bias.astype(BF16)


def head_terms(head, span, first, tile_rows, keys, values, bias, query_t, grad_t):
    size = query_t.shape[0]
    half, inside = head * size // LANES, head * size % LANES

    def alone(rows):
        parts = [jnp.zeros((inside, span), BF16)] if inside else []
        parts.append(rows)
        if inside + size < LANES:
            parts.append(jnp.zeros((LANES - inside - size, span), BF16))
        return jnp.concatenate(parts, axis=0)

    tile_of = (lax.broadcasted_iota(jnp.int32, (LANES, span), 1) + first) // tile_rows
    hot = (lax.broadcasted_iota(jnp.int32, (LANES, span), 0) == tile_of).astype(F32).astype(BF16)
    right = jnp.concatenate((alone(query_t), hot), axis=0)
    left = jnp.concatenate((keys[half], bias), axis=1)
    return dot(left, right, NN), dot(values[half], alone(grad_t), NN)


def chunk_of(ref, width):
    keys = [ref[:, k * LANES : (k + 1) * LANES] for k in range(width // LANES)]
    values = [ref[:, width + k * LANES : width + (k + 1) * LANES] for k in range(width // LANES)]
    return keys, values


def stats_of(ref, bias, query_t_ref, grad_t_ref, before_ref, stats_ref, span, tile_rows, factor):
    width, queries = query_t_ref.shape
    keys, values = chunk_of(ref, width)
    for head in range(H):
        rows = slice(head * width // H, (head + 1) * width // H)
        for first in range(0, queries, span):
            columns = slice(first, first + span)
            scores, dprobs = head_terms(
                head, span, first, tile_rows, keys, values, bias, query_t_ref[rows, columns], grad_t_ref[rows, columns]
            )
            top = jnp.max(scores, axis=0, keepdims=True)
            if before_ref is not None:
                old_top = before_ref[head : head + 1, columns]
                top = jnp.maximum(top, old_top)
            weights = jnp.exp2((scores - top) * factor)
            total = jnp.sum(weights, axis=0, keepdims=True)
            product = jnp.sum(weights * dprobs, axis=0, keepdims=True)
            if before_ref is not None:
                shrink = jnp.exp2((old_top - top) * factor)
                total = total + shrink * before_ref[H + head : H + head + 1, columns]
                product = product + shrink * before_ref[2 * H + head : 2 * H + head + 1, columns]
            stats_ref[head : head + 1, columns] = top
            stats_ref[H + head : H + head + 1, columns] = total
            stats_ref[2 * H + head : 2 * H + head + 1, columns] = product


def first_kernel(cams, masks, shard_rows, block_keys, span, tile_rows, factor, where_ref, query_ref, grad_ref, *refs):
    pieces, (chunk_ref, table_ref), outs = refs[:cams], refs[cams : cams + 2], refs[cams + 2 :]
    stats_ref, query_t_ref, grad_t_ref, bias_ref, far_ref = outs
    rows, _ = query_ref.shape
    build_bias(where_ref, table_ref, bias_ref, masks, shard_rows, block_keys)
    piece_rows = 2 * rows // cams
    for shift in range(cams):
        piece = lax.rem(where_ref[1] + cams - shift, cams)
        start = pl.multiple_of(piece * piece_rows, 16)
        far_ref[pl.ds(start, piece_rows), :] = pieces[shift][:piece_rows, :]
    query_t_ref[:, :rows] = query_ref[...].T
    query_t_ref[:, rows:] = far_ref[:rows, :].T
    grad_t_ref[:, :rows] = grad_ref[...].T
    grad_t_ref[:, rows:] = far_ref[rows:, :].T
    bias = bias_ref[: chunk_ref.shape[0], :]
    stats_of(chunk_ref, bias, query_t_ref, grad_t_ref, None, stats_ref, span, tile_rows, factor)


def second_kernel(span, tile_rows, factor, chunk_ref, bias_ref, query_t_ref, grad_t_ref, before_ref, stats_ref):
    bias = bias_ref[chunk_ref.shape[0] :, :]
    stats_of(chunk_ref, bias, query_t_ref, grad_t_ref, before_ref, stats_ref, span, tile_rows, factor)


def gradients(which, span, tile_rows, factor, scale, chunk_ref, bias_ref, query_t_ref, grad_t_ref, ends_ref, out_ref,
              query_sum_ref, before_ref, sums_ref):
    width, queries = query_t_ref.shape
    count = chunk_ref.shape[0]
    keys, values = chunk_of(chunk_ref, width)
    keys_t = chunk_ref[:, :width].T
    bias = bias_ref[which * count : (which + 1) * count, :]
    blocks = [(head, first) for head in range(H) for first in range(0, queries, span)]

    def rows_of(head):
        return slice(head * width // H, (head + 1) * width // H)

    def terms(head, first):
        rows, columns = rows_of(head), slice(first, first + span)
        return head_terms(
            head, span, first, tile_rows, keys, values, bias, query_t_ref[rows, columns], grad_t_ref[rows, columns]
        )

    def rounded(head, first, scores, dprobs):
        columns = slice(first, first + span)
        probs = jnp.exp2(scores * factor - ends_ref[head : head + 1, columns])
        dscores = (probs * (dprobs - ends_ref[H + head : H + head + 1, columns])).astype(BF16)
        return probs.astype(BF16), dscores

    def products(head, first, probs, dscores, sums):
        rows, columns = rows_of(head), slice(first, first + span)
        key_part = dot(query_t_ref[rows, columns], dscores, NT)
        value_part = dot(grad_t_ref[rows, columns], probs, NT)
        piece = dot(keys_t[rows, :], dscores, NN)
        if before_ref is not None:
            piece += before_ref[rows, columns]
        query_sum_ref[rows, columns] = piece
        sums = (key_part, value_part) if first == 0 else (sums[0] + key_part, sums[1] + value_part)
        if first + span == queries:
            sums_ref[rows, :] = sums[0] * scale
            sums_ref[width + rows.start : width + rows.stop, :] = sums[1]
        return sums

    ahead, lag = 1, 2
    raw, ready, sums = {}, {}, None
    for n in range(len(blocks) + ahead + lag):
        if n < len(blocks):
            raw[n] = terms(*blocks[n])
        if 0 <= n - ahead < len(blocks):
            ready[n - ahead] = rounded(*blocks[n - ahead], *raw.pop(n - ahead))
        if 0 <= n - ahead - lag:
            sums = products(*blocks[n - ahead - lag], *ready.pop(n - ahead - lag), sums)
    out_ref[...] = sums_ref[...].T.astype(out_ref.dtype)


def third_kernel(span, tile_rows, factor, scale, near_ref, across_ref, chunk_ref, bias_ref, query_t_ref, grad_t_ref,
                 out_ref, query_sum_ref, ends_ref, sums_ref):
    rows = near_ref.shape[1] // 2
    turned = jnp.concatenate((across_ref[:, rows:], across_ref[:, :rows]), axis=1)
    near_top, across_top = near_ref[:H, :], turned[:H, :]
    top = jnp.maximum(near_top, across_top)
    near, across = jnp.exp2((near_top - top) * factor), jnp.exp2((across_top - top) * factor)
    total = near * near_ref[H : 2 * H, :] + across * turned[H : 2 * H, :]
    product = near * near_ref[2 * H :, :] + across * turned[2 * H :, :]
    ends_ref[:H, :] = top * factor + jnp.log2(total)
    ends_ref[H:, :] = product / total
    gradients(1, span, tile_rows, factor, scale, chunk_ref, bias_ref, query_t_ref, grad_t_ref, ends_ref, out_ref,
              query_sum_ref, None, sums_ref)


def fourth_kernel(span, tile_rows, factor, scale, ends_ref, before_ref, chunk_ref, bias_ref, query_t_ref, grad_t_ref,
                  out_ref, own_ref, far_ref, query_sum_ref, sums_ref):
    gradients(0, span, tile_rows, factor, scale, chunk_ref, bias_ref, query_t_ref, grad_t_ref, ends_ref, out_ref,
              query_sum_ref, before_ref, sums_ref)
    rows = own_ref.shape[0]
    sums = query_sum_ref[...].T * scale
    own_ref[...] = sums[:rows, :]
    far_ref[...] = sums[rows:, :].astype(BF16)


def run(kernel, outs, args, scratch=(), smem=0, flops=0):
    size = lambda a: math.prod(a.shape) * a.dtype.itemsize
    moved = sum(size(a) for a in args) + sum(size(a) for a in outs)
    vmem = pl.BlockSpec(memory_space=pltpu.VMEM)
    return pl.pallas_call(
        kernel,
        out_shape=tuple(outs),
        in_specs=[pl.BlockSpec(memory_space=pltpu.SMEM)] * smem + [vmem] * (len(args) - smem),
        out_specs=tuple([vmem] * len(outs)),
        scratch_shapes=list(scratch),
        cost_estimate=pl.CostEstimate(flops=flops, bytes_accessed=moved, transcendentals=flops // 64),
        compiler_params=pltpu.CompilerParams(vmem_limit_bytes=40 * 1024 * 1024),
    )(*args)


def combine(parts, factor):
    top = functools.reduce(jnp.maximum, [part[:H] for part in parts])
    shrink = [jnp.exp2((part[:H] - top) * factor) for part in parts]
    total = sum(s * part[H : 2 * H] for s, part in zip(shrink, parts))
    product = sum(s * part[2 * H :] for s, part in zip(shrink, parts))
    return jnp.concatenate((top, total, product), axis=0)


def shards(queries, keys, values, grad_out, visible, counts):
    rows, width = queries.shape
    shard_rows = keys.shape[0]
    head_dim = width // H
    scale = 1.0 / math.sqrt(head_dim)
    factor = scale * math.log2(math.e)
    tiles, cams = lax.axis_size("tile"), lax.axis_size("cam")
    tile, cam = lax.axis_index("tile"), lax.axis_index("cam")
    blocks = counts.shape[0]
    block_keys = shard_rows * tiles // blocks
    own_tiles = visible.shape[0]
    tile_rows = rows // own_tiles
    orders = step_orders(tiles)
    masks = [slot_masks(order) for order in orders]
    span = 256

    def across(x, hop):
        pairs = [(c * tiles + t, c * tiles + (t ^ hop(c))) for c in range(cams) for t in range(tiles)]
        return lax.ppermute(x, ("cam", "tile"), pairs)

    def step(x, k):
        return across(x, lambda c: orders[c % 2][k])

    def swap_half(x):
        return across(x, lambda c: tiles // 2)

    def turn(x, shift):
        return lax.ppermute(x, "cam", [(c, (c + shift) % cams) for c in range(cams)])

    steps = len(orders[0])
    joined = jnp.concatenate((keys, values), axis=1)
    both = jnp.concatenate((queries, grad_out), axis=0)
    piece_rows = 2 * rows // cams
    mine = lax.dynamic_slice_in_dim(both, cam * piece_rows, piece_rows, 0)
    note = jnp.pad(visible.astype(BF16), ((0, 16 - own_tiles), (0, width - blocks)))
    received = swap_half(jnp.concatenate((mine, note), axis=0))
    held = joined
    for k in range(steps - 1):
        held = jnp.concatenate((held, step(held, k)), axis=0)
    pieces = [received] + [turn(received, shift) for shift in range(1, cams)]
    last = step(held, steps - 1)

    lanes = -(-blocks // LANES) * LANES
    own_seen = jnp.pad(visible.astype(BF16), ((0, 0), (0, lanes - blocks)))
    far_seen = jnp.pad(received[piece_rows : piece_rows + own_tiles, :blocks], ((0, 0), (0, lanes - blocks)))
    limit = jnp.pad(counts.astype(BF16)[None, :], ((0, 0), (0, lanes - blocks)))
    table = jnp.concatenate(
        (own_seen, far_seen, jnp.zeros((LANES - 1 - 2 * own_tiles, lanes), BF16), limit), axis=0
    )
    where = jnp.stack((tile, cam)).astype(jnp.int32)

    shape = jax.ShapeDtypeStruct
    all_rows = 2 * rows
    chunk = held.shape[0]
    work = 2 * all_rows * chunk * width
    stats, query_t, grad_t, bias = run(
        functools.partial(first_kernel, cams, masks, shard_rows, block_keys, span, tile_rows, factor),
        (
            shape((3 * H, all_rows), F32),
            shape((width, all_rows), BF16),
            shape((width, all_rows), BF16),
            shape((2 * chunk, LANES), BF16),
        ),
        (where, queries, grad_out, *pieces, held, table),
        scratch=(pltpu.VMEM((2 * rows, width), BF16),),
        smem=1,
        flops=8 * work,
    )
    (stats,) = run(
        functools.partial(second_kernel, span, tile_rows, factor),
        (shape((3 * H, all_rows), F32),),
        (last, bias, query_t, grad_t, stats),
        flops=8 * work,
    )
    near = combine([stats] + [turn(stats, shift) for shift in range(1, cams)], factor)
    opposite = swap_half(near)

    scratch = (pltpu.VMEM((2 * width, chunk), F32),)
    common = (bias, query_t, grad_t)
    sent, query_sum, ends = run(
        functools.partial(third_kernel, span, tile_rows, factor, scale),
        (shape((chunk, 2 * width), BF16), shape((width, all_rows), F32), shape((2 * H, all_rows), F32)),
        (near, opposite, last, *common),
        scratch=scratch,
        flops=20 * work,
    )
    got = step(sent, steps - 1)
    kept, query_own, query_far = run(
        functools.partial(fourth_kernel, span, tile_rows, factor, scale),
        (shape((chunk, 2 * width), F32), shape((rows, width), F32), shape((rows, width), BF16)),
        (ends, query_sum, held, *common),
        scratch=(pltpu.VMEM((width, all_rows), F32), *scratch),
        flops=20 * work,
    )
    query_got = swap_half(query_far)
    size = chunk
    for k in range(steps - 2, -1, -1):
        size //= 2
        out = (kept[size:] + got[size:].astype(F32)).astype(BF16)
        kept = kept[:size] + got[:size].astype(F32)
        got = step(out, k)
    owned = (kept + got.astype(F32)).astype(BF16)
    query_part = query_own + query_got.astype(F32)
    to_turn = query_part.astype(BF16)
    for shift in range(1, cams):
        query_part = query_part + turn(to_turn, shift).astype(F32)
    return (query_part.astype(BF16), owned[:, :width], owned[:, width:])


def solution(mesh):
    in_specs = (
        P("tile", None),
        P(("cam", "tile"), None),
        P(("cam", "tile"), None),
        P("tile", None),
        P("tile", "cam"),
        P("cam"),
    )
    out_specs = (P("tile", None), P(("cam", "tile"), None), P(("cam", "tile"), None))

    return jax.shard_map(shards, mesh=mesh, in_specs=in_specs, out_specs=out_specs, check_vma=False)
```

profile of v0, /device:TPU:0, one launch (start us, length us, event | category | flops | bytes accessed | tf_op | source)
XLA Modules:
  0.0 50.4 jit_solution(10488595509001870740)
XLA Ops:
  0.6 0.0 copy-start
  0.6 0.8 %constant_dynamic-update-slice_fusion.1 = bf16[64,512]{1,0:T(8,128)(2,1)S(1)} fusion(bf16[64,256]{1,0:T(8,128)(2,1)} %param.7), kind=kLoop, calls=%fused_computation.40 | loop fusion | bytes 65536
  1.4 0.8 %constant_dynamic-update-slice_fusion = bf16[64,512]{1,0:T(8,128)(2,1)S(1)} fusion(bf16[64,512]{1,0:T(8,128)(2,1)S(1)} %constant_dynamic-update-slice_fusion.1, bf16[64,256]{1,0:T(8,128)(2,1)} %param.8), kind=kLoop, calls=%fused_computation.39 | loop fusion | bytes 65536 | tf_op jit(solution)/shard_map/concatenate | solution.py:263
  2.2 3.1 %collective-permute-start = (bf16[64,512]{1,0:T(8,128)(2,1)S(1)}, bf16[64,512]{1,0:T(8,128)(2,1)S(1)}, u32[]{:S(2)}, u32[]{:S(2)}) collective-permute-start(bf16[64,512]{1,0:T(8,128)(2,1)S(1)} %constant_dynamic-update-slice_fusion), channel_id=1, source_target_pairs={{0,4},{1,5},{2,6},{3,7},{4,0},{5,1},{6,2},{7,3},{8,12},{9,13},{10,... | collective-permute-start | bytes 196616 | tf_op jit(solution)/shard_map/ppermute | solution.py:251
  5.2 0.0 copy-start.2
  5.3 0.7 %copy-done.2 = s32[2,32]{1,0:T(2,128)S(1)} copy-done((s32[2,32]{1,0:T(2,128)S(1)}, s32[2,32]{1,0:T(2,128)}, u32[]{:S(2)}) %copy-start.2) | copy-done | bytes 280
  5.9 0.0 copy-done
  5.9 0.1 fusion.3
  6.1 0.0 copy-start.3
  6.1 2.7 %collective-permute-start.3 = (bf16[272,256]{1,0:T(8,128)(2,1)S(1)}, bf16[272,256]{1,0:T(8,128)(2,1)S(1)}, u32[]{:S(2)}, u32[]{:S(2)}) collective-permute-start(bf16[272,256]{1,0:T(8,128)(2,1)S(1)} %fusion.2), channel_id=1, source_target_pairs={{0,8},{1,9},{2,10},{3,11},{4,12},{5,13},{6,14},{7,15},{8,0},{9,1},... | collective-permute-start | bytes 417800 | tf_op jit(solution)/shard_map/ppermute | solution.py:251
  8.8 0.0 collective-permute-done
  8.8 1.6 %collective-permute-start.1 = (bf16[128,512]{1,0:T(8,128)(2,1)S(1)}, bf16[128,512]{1,0:T(8,128)(2,1)S(1)}, u32[]{:S(2)}, u32[]{:S(2)}) collective-permute-start(bf16[128,512]{1,0:T(8,128)(2,1)S(1)} %pad_maximum_fusion.1), channel_id=1, source_target_pairs={{0,2},{1,3},{2,0},{3,1},{4,6},{5,7},{6,4},{7,5},{8,10},{9,11},{10,... | collective-permute-start | bytes 393224 | tf_op jit(solution)/shard_map/ppermute | solution.py:251
  10.4 0.0 copy-done.3
  10.4 0.1 pad.24.clone
  10.5 0.1 pad_add_fusion.where_ref
  10.5 5.5 %collective-permute-done.3.refs_0_ = bf16[272,256]{1,0:T(8,128)(2,1)S(1)} collective-permute-done((bf16[272,256]{1,0:T(8,128)(2,1)S(1)}, bf16[272,256]{1,0:T(8,128)(2,1)S(1)}, u32[]{:S(2)}, u32[]{:S(2)}) %collective-permute-start.3) | collective-permute-done | bytes 139296 | tf_op jit(solution)/shard_map/ppermute | solution.py:251
  16.0 0.0 copy-start.1
  16.0 0.0 collective-permute-start.4
  16.0 0.0 collective-permute-done.1
  16.1 0.6 %collective-permute-start.2 = (bf16[256,512]{1,0:T(8,128)(2,1)S(1)}, bf16[256,512]{1,0:T(8,128)(2,1)S(1)}, u32[]{:S(2)}, u32[]{:S(2)}) collective-permute-start(bf16[256,512]{1,0:T(8,128)(2,1)S(1)} %pad_maximum_fusion.refs_2_.chunk_ref), channel_id=1, source_target_pairs={{0,1},{1,0},{2,3},{3,2},{4,5},{5,4},{6,7},{7,6},{8,9},{9,8},{10,11... | collective-permute-start | bytes 786440 | tf_op jit(solution)/shard_map/ppermute | solution.py:251
  16.6 0.1 fusion.13.refs_3_
  16.7 0.7 %collective-permute-done.4.refs_1_ = bf16[272,256]{1,0:T(8,128)(2,1)S(1)} collective-permute-done((bf16[272,256]{1,0:T(8,128)(2,1)S(1)}, bf16[272,256]{1,0:T(8,128)(2,1)S(1)}, u32[]{:S(2)}, u32[]{:S(2)}) %collective-permute-start.4) | collective-permute-done | bytes 139296 | tf_op jit(solution)/shard_map/ppermute | solution.py:260
  17.4 0.0 copy-done.1
  17.4 2.1 %shard_map.85 = (f32[24,512]{1,0:T(8,128)S(1)}, bf16[256,512]{1,0:T(8,128)(2,1)S(1)}, bf16[256,512]{1,0:T(8,128)(2,1)S(1)}, bf16[512,128]{1,0:T(8,128)(2,1)S(1)}) custom-call(s32[2]{0:T(128)S(1)} %pad_add_fusion.where_ref, bf16[256,256]{1,0:T(8,128)(2,1)S(1)} %copy-done, bf16[256,256]{1,0:T(8,128)(2,1)S(1)} %copy-done.1, ...), custom_call_target="tpu_custom_call" | custom-call | flops 536870912 | bytes 1540104 | tf_op jit(solution)/shard_map/pallas_call | solution.py:214
  19.5 3.0 %collective-permute-done.2.chunk_ref = bf16[256,512]{1,0:T(8,128)(2,1)S(1)} collective-permute-done((bf16[256,512]{1,0:T(8,128)(2,1)S(1)}, bf16[256,512]{1,0:T(8,128)(2,1)S(1)}, u32[]{:S(2)}, u32[]{:S(2)}) %collective-permute-start.2) | collective-permute-done | bytes 262176 | tf_op jit(solution)/shard_map/ppermute | solution.py:251
  22.5 1.5 %shard_map.86 = f32[24,512]{1,0:T(8,128)S(1)} custom-call(bf16[256,512]{1,0:T(8,128)(2,1)S(1)} %collective-permute-done.2.chunk_ref, bf16[512,128]{1,0:T(8,128)(2,1)S(1)} %get-tuple-element.13.bias_ref, bf16[256,512]{1,0:T(8,128)(2,1)S(1)} %get-tuple-element.14.query_t_ref, bf16[256,512]{1,0:T(8,128)(2,1)S(1)} %get-tuple-element.15.grad_t_ref, ...), custom_call_target="tpu_custom_call" | custom-call | flops 536870912 | bytes 1015808 | tf_op jit(solution)/shard_map/pallas_call | solution.py:214
  24.0 0.1 collective-permute-start.5
  24.1 1.2 %collective-permute-done.5 = f32[24,512]{1,0:T(8,128)S(1)} collective-permute-done((f32[24,512]{1,0:T(8,128)S(1)}, f32[24,512]{1,0:T(8,128)S(1)}, u32[]{:S(2)}, u32[]{:S(2)}) %collective-permute-start.5) | collective-permute-done | bytes 49184 | tf_op jit(solution)/shard_map/ppermute | solution.py:260
  25.4 0.3 collective-permute-start.6
  25.7 5.5 %collective-permute-done.6.across_ref = f32[24,512]{1,0:T(8,128)S(1)} collective-permute-done((f32[24,512]{1,0:T(8,128)S(1)}, f32[24,512]{1,0:T(8,128)S(1)}, u32[]{:S(2)}, u32[]{:S(2)}) %collective-permute-start.6) | collective-permute-done | bytes 49184 | tf_op jit(solution)/shard_map/ppermute | solution.py:251
  31.2 2.4 %shard_map.87 = (bf16[256,512]{1,0:T(8,128)(2,1)S(1)}, f32[256,512]{1,0:T(8,128)S(1)}, f32[16,512]{1,0:T(8,128)S(1)}) custom-call(f32[24,512]{1,0:T(8,128)S(1)} %pad_maximum_fusion.2.near_ref, f32[24,512]{1,0:T(8,128)S(1)} %collective-permute-done.6.across_ref, bf16[256,512]{1,0:T(8,128)(2,1)S(1)} %collective-permute-done.2.chunk_ref, ...), custom_call_target="tpu_custom_call" | custom-call | flops 1342177280 | bytes 1835008 | tf_op jit(solution)/shard_map/pallas_call | solution.py:214
  33.6 0.8 %collective-permute-start.9 = (bf16[256,512]{1,0:T(8,128)(2,1)S(1)}, bf16[256,512]{1,0:T(8,128)(2,1)S(1)}, u32[]{:S(2)}, u32[]{:S(2)}) collective-permute-start(bf16[256,512]{1,0:T(8,128)(2,1)S(1)} %get-tuple-element.22), channel_id=1, source_target_pairs={{0,1},{1,0},{2,3},{3,2},{4,5},{5,4},{6,7},{7,6},{8,9},{9,8},{10,11... | collective-permute-start | bytes 786440 | tf_op jit(solution)/shard_map/ppermute | solution.py:251
  34.5 2.5 %shard_map.88 = (f32[256,512]{1,0:T(8,128)S(1)}, f32[256,256]{1,0:T(8,128)S(1)}, bf16[256,256]{1,0:T(8,128)(2,1)S(1)}) custom-call(f32[16,512]{1,0:T(8,128)S(1)} %get-tuple-element.17.ends_ref, f32[256,512]{1,0:T(8,128)S(1)} %get-tuple-element.18.before_ref, bf16[256,512]{1,0:T(8,128)(2,1)S(1)} %pad_maximum_fusion.refs_2_.chunk_ref, ...), custom_call_target="tpu_custom_call" | custom-call | flops 1342177280 | bytes 2392064 | tf_op jit(solution)/shard_map/pallas_call | solution.py:214
  37.0 0.1 collective-permute-start.7
  37.0 3.1 %collective-permute-done.9 = bf16[256,512]{1,0:T(8,128)(2,1)S(1)} collective-permute-done((bf16[256,512]{1,0:T(8,128)(2,1)S(1)}, bf16[256,512]{1,0:T(8,128)(2,1)S(1)}, u32[]{:S(2)}, u32[]{:S(2)}) %collective-permute-start.9) | collective-permute-done | bytes 262176 | tf_op jit(solution)/shard_map/ppermute | solution.py:251
  40.1 0.1 add_convert_fusion
  40.2 1.6 %collective-permute-start.10 = (bf16[128,512]{1,0:T(8,128)(2,1)S(1)}, bf16[128,512]{1,0:T(8,128)(2,1)S(1)}, u32[]{:S(2)}, u32[]{:S(2)}) collective-permute-start(bf16[128,512]{1,0:T(8,128)(2,1)S(1)} %get-tuple-element.25), channel_id=1, source_target_pairs={{0,2},{1,3},{2,0},{3,1},{4,6},{5,7},{6,4},{7,5},{8,10},{9,11},{10,... | collective-permute-start | bytes 393224 | tf_op jit(solution)/shard_map/ppermute | solution.py:251
  41.7 3.6 %collective-permute-done.7 = bf16[256,256]{1,0:T(8,128)(2,1)S(1)} collective-permute-done((bf16[256,256]{1,0:T(8,128)(2,1)S(1)}, bf16[256,256]{1,0:T(8,128)(2,1)S(1)}, u32[]{:S(2)}, u32[]{:S(2)}) %collective-permute-start.7) | collective-permute-done | bytes 131104 | tf_op jit(solution)/shard_map/ppermute | solution.py:251
  45.3 0.1 collective-permute-start.8
  45.4 0.0 collective-permute-done.10
  45.4 0.1 collective-permute-start.11
  45.5 1.2 %collective-permute-done.8 = bf16[256,256]{1,0:T(8,128)(2,1)S(1)} collective-permute-done((bf16[256,256]{1,0:T(8,128)(2,1)S(1)}, bf16[256,256]{1,0:T(8,128)(2,1)S(1)}, u32[]{:S(2)}, u32[]{:S(2)}) %collective-permute-start.8) | collective-permute-done | bytes 131104 | tf_op jit(solution)/shard_map/ppermute | solution.py:260
  46.7 0.7 %add_convert_fusion.1 = bf16[256,256]{1,0:T(8,128)(2,1)} fusion(bf16[256,256]{1,0:T(8,128)(2,1)S(1)} %collective-permute-done.8, f32[256,256]{1,0:T(8,128)S(1)} %get-tuple-element.19, bf16[256,256]{1,0:T(8,128)(2,1)S(1)} %collective-permute-done.7), kind=kLoop, calls=%fused_computation.7 | loop fusion | flops 327680 | bytes 655360 | tf_op jit(solution)/shard_map/convert_element_type | solution.py:339
  47.4 2.3 %collective-permute-done.11 = bf16[64,512]{1,0:T(8,128)(2,1)S(1)} collective-permute-done((bf16[64,512]{1,0:T(8,128)(2,1)S(1)}, bf16[64,512]{1,0:T(8,128)(2,1)S(1)}, u32[]{:S(2)}, u32[]{:S(2)}) %collective-permute-start.11) | collective-permute-done | bytes 65568 | tf_op jit(solution)/shard_map/ppermute | solution.py:251
  49.8 0.6 %fusion.16 = (bf16[64,256]{1,0:T(8,128)(2,1)}, bf16[64,256]{1,0:T(8,128)(2,1)}) fusion(bf16[64,512]{1,0:T(8,128)(2,1)S(1)} %fusion.6), kind=kLoop, calls=%fused_computation.43 | loop fusion | bytes 131072 | tf_op jit(solution)/shard_map/slice | solution.py:339
  (13 shorter events, 0.2 us)
Async XLA Ops:
  0.6 5.3 %copy-start = (bf16[256,256]{1,0:T(8,128)(2,1)S(1)}, bf16[256,256]{1,0:T(8,128)(2,1)}, u32[]{:S(2)}) copy-start(bf16[256,256]{1,0:T(8,128)(2,1)} %query_ref.1) | copy-start | bytes 393220
  2.2 6.6 %collective-permute-start = (bf16[64,512]{1,0:T(8,128)(2,1)S(1)}, bf16[64,512]{1,0:T(8,128)(2,1)S(1)}, u32[]{:S(2)}, u32[]{:S(2)}) collective-permute-start(bf16[64,512]{1,0:T(8,128)(2,1)S(1)} %constant_dynamic-update-slice_fusion), channel_id=1, source_target_pairs={{0,4},{1,5},{2,6},{3,7},{4,0},{5,1},{6,2},{7,3},{8,12},{9,13},{10,... | collective-permute-start | bytes 196616 | tf_op jit(solution)/shard_map/ppermute | solution.py:251
  5.2 0.7 %copy-start.2 = (s32[2,32]{1,0:T(2,128)S(1)}, s32[2,32]{1,0:T(2,128)}, u32[]{:S(2)}) copy-start(s32[2,32]{1,0:T(2,128)} %param.10) | copy-start | bytes 772
  6.1 4.3 %copy-start.3 = (s32[32]{0:T(128)S(1)}, s32[32]{0:T(128)}, u32[]{:S(2)}) copy-start(s32[32]{0:T(128)} %param.11) | copy-start | bytes 388
  6.1 9.9 %collective-permute-start.3 = (bf16[272,256]{1,0:T(8,128)(2,1)S(1)}, bf16[272,256]{1,0:T(8,128)(2,1)S(1)}, u32[]{:S(2)}, u32[]{:S(2)}) collective-permute-start(bf16[272,256]{1,0:T(8,128)(2,1)S(1)} %fusion.2), channel_id=1, source_target_pairs={{0,8},{1,9},{2,10},{3,11},{4,12},{5,13},{6,14},{7,15},{8,0},{9,1},... | collective-permute-start | bytes 417800 | tf_op jit(solution)/shard_map/ppermute | solution.py:251
  8.8 7.2 %collective-permute-start.1 = (bf16[128,512]{1,0:T(8,128)(2,1)S(1)}, bf16[128,512]{1,0:T(8,128)(2,1)S(1)}, u32[]{:S(2)}, u32[]{:S(2)}) collective-permute-start(bf16[128,512]{1,0:T(8,128)(2,1)S(1)} %pad_maximum_fusion.1), channel_id=1, source_target_pairs={{0,2},{1,3},{2,0},{3,1},{4,6},{5,7},{6,4},{7,5},{8,10},{9,11},{10,... | collective-permute-start | bytes 393224 | tf_op jit(solution)/shard_map/ppermute | solution.py:251
  16.0 1.4 %copy-start.1 = (bf16[256,256]{1,0:T(8,128)(2,1)S(1)}, bf16[256,256]{1,0:T(8,128)(2,1)}, u32[]{:S(2)}) copy-start(bf16[256,256]{1,0:T(8,128)(2,1)} %grad_ref.1) | copy-start | bytes 393220
  16.0 1.4 %collective-permute-start.4 = (bf16[272,256]{1,0:T(8,128)(2,1)S(1)}, bf16[272,256]{1,0:T(8,128)(2,1)S(1)}, u32[]{:S(2)}, u32[]{:S(2)}) collective-permute-start(bf16[272,256]{1,0:T(8,128)(2,1)S(1)} %collective-permute-done.3.refs_0_), channel_id=1, source_target_pairs={{0,16},{16,0},{1,17},{17,1},{2,18},{18,2},{3,19},{19,3},{4,20},{20... | collective-permute-start | bytes 417800 | tf_op jit(solution)/shard_map/ppermute | solution.py:260
  16.1 6.4 %collective-permute-start.2 = (bf16[256,512]{1,0:T(8,128)(2,1)S(1)}, bf16[256,512]{1,0:T(8,128)(2,1)S(1)}, u32[]{:S(2)}, u32[]{:S(2)}) collective-permute-start(bf16[256,512]{1,0:T(8,128)(2,1)S(1)} %pad_maximum_fusion.refs_2_.chunk_ref), channel_id=1, source_target_pairs={{0,1},{1,0},{2,3},{3,2},{4,5},{5,4},{6,7},{7,6},{8,9},{9,8},{10,11... | collective-permute-start | bytes 786440 | tf_op jit(solution)/shard_map/ppermute | solution.py:251
  24.0 1.3 %collective-permute-start.5 = (f32[24,512]{1,0:T(8,128)S(1)}, f32[24,512]{1,0:T(8,128)S(1)}, u32[]{:S(2)}, u32[]{:S(2)}) collective-permute-start(f32[24,512]{1,0:T(8,128)S(1)} %shard_map.86), channel_id=1, source_target_pairs={{0,16},{16,0},{1,17},{17,1},{2,18},{18,2},{3,19},{19,3},{4,20},{20... | collective-permute-start | bytes 147464 | tf_op jit(solution)/shard_map/ppermute | solution.py:260
  25.4 5.8 %collective-permute-start.6 = (f32[24,512]{1,0:T(8,128)S(1)}, f32[24,512]{1,0:T(8,128)S(1)}, u32[]{:S(2)}, u32[]{:S(2)}) collective-permute-start(f32[24,512]{1,0:T(8,128)S(1)} %pad_maximum_fusion.2.near_ref), channel_id=1, source_target_pairs={{0,8},{1,9},{2,10},{3,11},{4,12},{5,13},{6,14},{7,15},{8,0},{9,1},... | collective-permute-start | bytes 147464 | tf_op jit(solution)/shard_map/ppermute | solution.py:251
  33.6 6.4 %collective-permute-start.9 = (bf16[256,512]{1,0:T(8,128)(2,1)S(1)}, bf16[256,512]{1,0:T(8,128)(2,1)S(1)}, u32[]{:S(2)}, u32[]{:S(2)}) collective-permute-start(bf16[256,512]{1,0:T(8,128)(2,1)S(1)} %get-tuple-element.22), channel_id=1, source_target_pairs={{0,1},{1,0},{2,3},{3,2},{4,5},{5,4},{6,7},{7,6},{8,9},{9,8},{10,11... | collective-permute-start | bytes 786440 | tf_op jit(solution)/shard_map/ppermute | solution.py:251
  37.0 8.3 %collective-permute-start.7 = (bf16[256,256]{1,0:T(8,128)(2,1)S(1)}, bf16[256,256]{1,0:T(8,128)(2,1)S(1)}, u32[]{:S(2)}, u32[]{:S(2)}) collective-permute-start(bf16[256,256]{1,0:T(8,128)(2,1)S(1)} %get-tuple-element.20), channel_id=1, source_target_pairs={{0,8},{1,9},{2,10},{3,11},{4,12},{5,13},{6,14},{7,15},{8,0},{9,1},... | collective-permute-start | bytes 393224 | tf_op jit(solution)/shard_map/ppermute | solution.py:251
  40.2 5.2 %collective-permute-start.10 = (bf16[128,512]{1,0:T(8,128)(2,1)S(1)}, bf16[128,512]{1,0:T(8,128)(2,1)S(1)}, u32[]{:S(2)}, u32[]{:S(2)}) collective-permute-start(bf16[128,512]{1,0:T(8,128)(2,1)S(1)} %get-tuple-element.25), channel_id=1, source_target_pairs={{0,2},{1,3},{2,0},{3,1},{4,6},{5,7},{6,4},{7,5},{8,10},{9,11},{10,... | collective-permute-start | bytes 393224 | tf_op jit(solution)/shard_map/ppermute | solution.py:251
  45.3 1.4 %collective-permute-start.8 = (bf16[256,256]{1,0:T(8,128)(2,1)S(1)}, bf16[256,256]{1,0:T(8,128)(2,1)S(1)}, u32[]{:S(2)}, u32[]{:S(2)}) collective-permute-start(bf16[256,256]{1,0:T(8,128)(2,1)S(1)} %fusion.1), channel_id=1, source_target_pairs={{0,16},{16,0},{1,17},{17,1},{2,18},{18,2},{3,19},{19,3},{4,20},{20... | collective-permute-start | bytes 393224 | tf_op jit(solution)/shard_map/ppermute | solution.py:260
  45.4 4.3 %collective-permute-start.11 = (bf16[64,512]{1,0:T(8,128)(2,1)S(1)}, bf16[64,512]{1,0:T(8,128)(2,1)S(1)}, u32[]{:S(2)}, u32[]{:S(2)}) collective-permute-start(bf16[64,512]{1,0:T(8,128)(2,1)S(1)} %fusion.4), channel_id=1, source_target_pairs={{0,4},{1,5},{2,6},{3,7},{4,0},{5,1},{6,2},{7,3},{8,12},{9,13},{10,... | collective-permute-start | bytes 196616 | tf_op jit(solution)/shard_map/ppermute | solution.py:251
where the time goes:
time: 50.6 us; the launch traced here: 50.4 us
  waiting for transfers between devices  26 us (51%)
  starting transfers between devices  10.9 us (22%)
  Pallas kernels  8.58 us (17%)
  local copies, waits for them, and re-layouts  2.96 us (6%)
  other arithmetic  1.22 us (2%)
  between operations  0.8 us (2%)
    ppermute x9, waiting for transfers between devices, across(): return lax.ppermute(x, ('cam', 'tile'), pairs)  22.9 us
    ppermute x9, starting transfers between devices, across(): return lax.ppermute(x, ('cam', 'tile'), pairs)  10.7 us
    pallas_call x4, Pallas kernels, run(): pl.pallas_call(kernel, out_shape=tuple(outs), in_specs=[pl.BlockSpec(memo...  8.58 us
    ppermute x3, waiting for transfers between devices, turn(): lax.ppermute(x, 'cam', [(c, (c + shift) % cams) for c in range(cams)])  3.13 us
    unnamed x9, local copies, waits for them, and re-layouts  1.49 us
  transfers between devices with their start and end apart: 12, of which 9 were waited for; matrix products, arithmetic and copies ran while one was open for 2% of the time, Pallas kernels for 9%

commit v1 on v0

v1 whole, which is shorter than its diff:
```python
import functools
import math

import jax
import jax.numpy as jnp
from jax import lax
from jax.experimental import pallas as pl
from jax.experimental.pallas import tpu as pltpu
from jax.sharding import PartitionSpec as P


H = 8
LANES = 128
FAR = -1e30
BF16 = jnp.bfloat16
F32 = jnp.float32


def dot(a, b, dims):
    return lax.dot_general(a, b, (dims, ((), ())), preferred_element_type=F32)


NN = ((1,), (0,))
NT = ((1,), (1,))


def step_orders(tiles):
    bits = []
    bit = 1
    while bit < tiles // 2:
        bits.append(bit)
        bit *= 2
    return (tuple(bits[::-1]), tuple(bits[:1:-1] + bits[:2]))


def slot_masks(order):
    masks = [0]
    for bit in order:
        masks = masks + [mask ^ bit for mask in masks]
    return masks


def start_kernel(cams, where_ref, key_ref, value_ref, query_ref, grad_ref, seen_ref, limit_ref, pair_ref, query_out,
                 grad_out, message_ref, table_ref, seen_vmem, limit_vmem, sems):
    rows, width = query_ref.shape
    own_tiles, blocks = seen_ref.shape
    moves = (
        (query_ref, query_out),
        (grad_ref, grad_out),
        (seen_ref, seen_vmem),
        (limit_ref, limit_vmem),
        (key_ref, pair_ref.at[:, :width]),
        (value_ref, pair_ref.at[:, width:]),
    )
    copies = [pltpu.make_async_copy(source, target, sems.at[k]) for k, (source, target) in enumerate(moves)]
    for copy in copies:
        copy.start()
    piece_rows = 2 * rows // cams
    message_ref[piece_rows:, :] = jnp.zeros((16, width), BF16)
    table_ref[...] = jnp.zeros(table_ref.shape, BF16)
    for copy in copies:
        copy.wait()
    for piece in range(cams):

        @pl.when(where_ref[1] == piece)
        def _(first=piece * piece_rows):
            source, at = (query_out, first) if first < rows else (grad_out, first - rows)
            message_ref[:piece_rows, :] = source[at : at + piece_rows, :]

    seen = seen_vmem[...].astype(F32).astype(BF16)
    message_ref[piece_rows : piece_rows + own_tiles, :blocks] = seen
    table_ref[:own_tiles, :blocks] = seen
    table_ref[LANES - 1 : LANES, :blocks] = limit_vmem[...].astype(F32).astype(BF16)


def build_bias(where_ref, table_ref, bias_ref, masks, shard_rows, block_keys):
    tile, cam = where_ref[0], where_ref[1]
    per_shard = shard_rows // block_keys
    lanes = table_ref.shape[1]
    table = table_ref[...]
    lane = lax.broadcasted_iota(jnp.int32, (shard_rows, lanes), 1)
    row = lax.broadcasted_iota(jnp.int32, (shard_rows, lanes), 0)
    place = lax.broadcasted_iota(jnp.int32, (shard_rows, LANES), 0) % block_keys
    column = lax.broadcasted_iota(jnp.int32, (shard_rows, LANES), 1)
    for slot in range(len(masks[0])):
        mask = jnp.where(cam % 2 == 0, masks[0][slot], masks[1][slot])
        block = (tile ^ mask) * per_shard + row // block_keys
        picked = dot((lane == block).astype(F32).astype(BF16), table, NT)
        count = picked[:, LANES - 1 : LANES]
        allowed = (picked > 0.5) & (place.astype(F32) < count)
        bias = jnp.where(allowed | (column == LANES - 1), 0.0, FAR)
        bias_ref[slot * shard_rows : (slot + 1) * shard_rows, :] = bias.astype(BF16)


def head_terms(head, span, first, tile_rows, keys, values, bias, query_t, grad_t):
    size = query_t.shape[0]
    half, inside = head * size // LANES, head * size % LANES

    def alone(rows):
        parts = [jnp.zeros((inside, span), BF16)] if inside else []
        parts.append(rows)
        if inside + size < LANES:
            parts.append(jnp.zeros((LANES - inside - size, span), BF16))
        return jnp.concatenate(parts, axis=0)

    tile_of = (lax.broadcasted_iota(jnp.int32, (LANES, span), 1) + first) // tile_rows
    hot = (lax.broadcasted_iota(jnp.int32, (LANES, span), 0) == tile_of).astype(F32).astype(BF16)
    right = jnp.concatenate((alone(query_t), hot), axis=0)
    left = jnp.concatenate((keys[half], bias), axis=1)
    return dot(left, right, NN), dot(values[half], alone(grad_t), NN)


def chunk_of(ref, width):
    keys = [ref[:, k * LANES : (k + 1) * LANES] for k in range(width // LANES)]
    values = [ref[:, width + k * LANES : width + (k + 1) * LANES] for k in range(width // LANES)]
    return keys, values


def stats_of(ref, bias, query_t_ref, grad_t_ref, before_ref, stats_ref, span, tile_rows, factor):
    width, queries = query_t_ref.shape
    keys, values = chunk_of(ref, width)
    for head in range(H):
        rows = slice(head * width // H, (head + 1) * width // H)
        for first in range(0, queries, span):
            columns = slice(first, first + span)
            scores, dprobs = head_terms(
                head, span, first, tile_rows, keys, values, bias, query_t_ref[rows, columns], grad_t_ref[rows, columns]
            )
            top = jnp.max(scores, axis=0, keepdims=True)
            if before_ref is not None:
                old_top = before_ref[head : head + 1, columns]
                top = jnp.maximum(top, old_top)
            weights = jnp.exp2((scores - top) * factor)
            total = jnp.sum(weights, axis=0, keepdims=True)
            product = jnp.sum(weights * dprobs, axis=0, keepdims=True)
            if before_ref is not None:
                shrink = jnp.exp2((old_top - top) * factor)
                total = total + shrink * before_ref[H + head : H + head + 1, columns]
                product = product + shrink * before_ref[2 * H + head : 2 * H + head + 1, columns]
            stats_ref[head : head + 1, columns] = top
            stats_ref[H + head : H + head + 1, columns] = total
            stats_ref[2 * H + head : 2 * H + head + 1, columns] = product


def first_kernel(cams, blocks, masks, shard_rows, block_keys, span, tile_rows, factor, where_ref, query_ref, grad_ref, *refs):
    pieces, (chunk_ref, table_ref), outs = refs[:cams], refs[cams : cams + 2], refs[cams + 2 :]
    stats_ref, query_t_ref, grad_t_ref, bias_ref, far_ref, full_table_ref = outs
    rows, _ = query_ref.shape
    own_tiles = rows // tile_rows
    note = slice(2 * rows // cams, 2 * rows // cams + own_tiles)
    full_table_ref[...] = table_ref[...]
    full_table_ref[own_tiles : 2 * own_tiles, :blocks] = pieces[0][note, :blocks]
    build_bias(where_ref, full_table_ref, bias_ref, masks, shard_rows, block_keys)
    piece_rows = 2 * rows // cams
    for shift in range(cams):
        piece = lax.rem(where_ref[1] + cams - shift, cams)
        start = pl.multiple_of(piece * piece_rows, 16)
        far_ref[pl.ds(start, piece_rows), :] = pieces[shift][:piece_rows, :]
    query_t_ref[:, :rows] = query_ref[...].T
    query_t_ref[:, rows:] = far_ref[:rows, :].T
    grad_t_ref[:, :rows] = grad_ref[...].T
    grad_t_ref[:, rows:] = far_ref[rows:, :].T
    bias = bias_ref[: chunk_ref.shape[0], :]
    stats_of(chunk_ref, bias, query_t_ref, grad_t_ref, None, stats_ref, span, tile_rows, factor)


def second_kernel(span, tile_rows, factor, chunk_ref, bias_ref, query_t_ref, grad_t_ref, before_ref, stats_ref):
    bias = bias_ref[chunk_ref.shape[0] :, :]
    stats_of(chunk_ref, bias, query_t_ref, grad_t_ref, before_ref, stats_ref, span, tile_rows, factor)


def head_rows(head, width):
    return slice(head * width // H, (head + 1) * width // H)


def staggered(count, stages, lags):
    results = [{} for _ in stages]
    total = sum(lags)
    for n in range(count + total):
        at = n
        for k, stage in enumerate(stages):
            at -= lags[k]
            if 0 <= at < count:
                results[k][at] = stage(at) if k == 0 else stage(at, results[k - 1].pop(at))


def block_list(queries, span):
    return [(head, slice(first, first + span)) for head in range(H) for first in range(0, queries, span)]


def near_kernel(span, tile_rows, factor, near_ref, chunk_ref, bias_ref, query_t_ref, grad_t_ref, weights_ref, dprobs_ref):
    width, queries = query_t_ref.shape
    keys, values = chunk_of(chunk_ref, width)
    bias = bias_ref[chunk_ref.shape[0] :, :]
    blocks = block_list(queries, span)

    def terms(n):
        head, columns = blocks[n]
        rows = head_rows(head, width)
        return head_terms(
            head, span, columns.start, tile_rows, keys, values, bias, query_t_ref[rows, columns], grad_t_ref[rows, columns]
        )

    def store(n, raw):
        head, columns = blocks[n]
        place = slice(n * span, (n + 1) * span)
        weights_ref[:, place] = jnp.exp2(raw[0] * factor - near_ref[head : head + 1, columns])
        dprobs_ref[:, place] = raw[1]

    staggered(len(blocks), (terms, store), (0, 1))


def products_of(blocks, queries, query_t_ref, grad_t_ref, keys_t, query_sum_ref, before_ref, sums_ref, scale):
    width = query_t_ref.shape[0]
    partial = {}

    def products(n, ready):
        head, columns = blocks[n]
        probs, dscores = ready
        rows = head_rows(head, width)
        key_part = dot(query_t_ref[rows, columns], dscores, NT)
        value_part = dot(grad_t_ref[rows, columns], probs, NT)
        piece = dot(keys_t[rows, :], dscores, NN)
        if before_ref is not None:
            piece += before_ref[rows, columns]
        query_sum_ref[rows, columns] = piece
        if columns.start > 0:
            before = partial.pop(head)
            key_part, value_part = before[0] + key_part, before[1] + value_part
        if columns.stop < queries:
            partial[head] = (key_part, value_part)
        else:
            sums_ref[rows, :] = key_part * scale
            sums_ref[width + rows.start : width + rows.stop, :] = value_part

    return products


def third_kernel(span, scale, near_ref, across_ref, chunk_ref, query_t_ref, grad_t_ref, weights_ref, dprobs_ref,
                 out_ref, query_sum_ref, ends_ref, sums_ref, shrink_ref):
    width, queries = query_t_ref.shape
    rows = queries // 2
    turned = jnp.concatenate((across_ref[:, rows:], across_ref[:, :rows]), axis=1)
    top = jnp.maximum(near_ref[:H, :], turned[:H, :])
    near, across = jnp.exp2(near_ref[:H, :] - top), jnp.exp2(turned[:H, :] - top)
    total = near + across
    lse = top + jnp.log2(total)
    ends_ref[:H, :] = lse
    ends_ref[H:, :] = (near * near_ref[H:, :] + across * turned[H:, :]) / total
    shrink_ref[...] = jnp.exp2(near_ref[:H, :] - lse)
    keys_t = chunk_ref[:, :width].T
    blocks = block_list(queries, span)

    def rounded(n):
        head, columns = blocks[n]
        place = slice(n * span, (n + 1) * span)
        probs = weights_ref[:, place] * shrink_ref[head : head + 1, columns]
        dscores = probs * (dprobs_ref[:, place] - ends_ref[H + head : H + head + 1, columns])
        return probs.astype(BF16), dscores.astype(BF16)

    products = products_of(blocks, queries, query_t_ref, grad_t_ref, keys_t, query_sum_ref, None, sums_ref, scale)
    staggered(len(blocks), (rounded, products), (0, 1))
    out_ref[...] = sums_ref[...].T.astype(out_ref.dtype)


def fourth_kernel(cams, span, tile_rows, factor, scale, where_ref, ends_ref, before_ref, chunk_ref, bias_ref, query_t_ref,
                  grad_t_ref, out_ref, keep_ref, *refs):
    turn_refs, (query_sum_ref, sums_ref, whole_ref) = refs[: cams - 1], refs[cams - 1 :]
    width, queries = query_t_ref.shape
    keys, values = chunk_of(chunk_ref, width)
    keys_t = chunk_ref[:, :width].T
    bias = bias_ref[: chunk_ref.shape[0], :]
    blocks = block_list(queries, span)

    def terms(n):
        head, columns = blocks[n]
        rows = head_rows(head, width)
        return head_terms(
            head, span, columns.start, tile_rows, keys, values, bias, query_t_ref[rows, columns], grad_t_ref[rows, columns]
        )

    def rounded(n, raw):
        head, columns = blocks[n]
        probs = jnp.exp2(raw[0] * factor - ends_ref[head : head + 1, columns])
        dscores = probs * (raw[1] - ends_ref[H + head : H + head + 1, columns])
        return probs.astype(BF16), dscores.astype(BF16)

    products = products_of(blocks, queries, query_t_ref, grad_t_ref, keys_t, query_sum_ref, before_ref, sums_ref, scale)
    staggered(len(blocks), (terms, rounded, products), (0, 1, 2))
    out_ref[...] = sums_ref[...].T.astype(out_ref.dtype)
    whole_ref[...] = query_sum_ref[...].T * scale
    count = keep_ref.shape[0] // 2
    for shift, ref in enumerate((keep_ref, *turn_refs)):
        piece = lax.rem(where_ref[1] + shift, cams)
        for side in range(2):
            start = pl.multiple_of(side * (queries // 2) + piece * count, 16)
            ref[side * count : (side + 1) * count, :] = whole_ref[pl.ds(start, count), :].astype(ref.dtype)


def run(kernel, outs, args, scratch=(), smem=0, flops=0, space=pltpu.VMEM):
    size = lambda a: math.prod(a.shape) * a.dtype.itemsize
    moved = sum(size(a) for a in args) + sum(size(a) for a in outs)
    vmem = pl.BlockSpec(memory_space=pltpu.VMEM)
    return pl.pallas_call(
        kernel,
        out_shape=tuple(outs),
        in_specs=[pl.BlockSpec(memory_space=pltpu.SMEM)] * smem + [pl.BlockSpec(memory_space=space)] * (len(args) - smem),
        out_specs=tuple([vmem] * len(outs)),
        scratch_shapes=list(scratch),
        cost_estimate=pl.CostEstimate(flops=flops, bytes_accessed=moved, transcendentals=flops // 64),
        compiler_params=pltpu.CompilerParams(vmem_limit_bytes=40 * 1024 * 1024),
    )(*args)


def combine(parts, factor):
    top = functools.reduce(jnp.maximum, [part[:H] for part in parts])
    shrink = [jnp.exp2((part[:H] - top) * factor) for part in parts]
    total = sum(s * part[H : 2 * H] for s, part in zip(shrink, parts))
    product = sum(s * part[2 * H :] for s, part in zip(shrink, parts))
    return jnp.concatenate((top * factor + jnp.log2(total), product / total), axis=0)


def shards(queries, keys, values, grad_out, visible, counts):
    rows, width = queries.shape
    shard_rows = keys.shape[0]
    head_dim = width // H
    scale = 1.0 / math.sqrt(head_dim)
    factor = scale * math.log2(math.e)
    tiles, cams = lax.axis_size("tile"), lax.axis_size("cam")
    tile, cam = lax.axis_index("tile"), lax.axis_index("cam")
    blocks = counts.shape[0]
    block_keys = shard_rows * tiles // blocks
    own_tiles = visible.shape[0]
    tile_rows = rows // own_tiles
    orders = step_orders(tiles)
    masks = [slot_masks(order) for order in orders]
    span = 256

    def across(x, hop):
        pairs = [(c * tiles + t, c * tiles + (t ^ hop(c))) for c in range(cams) for t in range(tiles)]
        return lax.ppermute(x, ("cam", "tile"), pairs)

    def step(x, k):
        return across(x, lambda c: orders[c % 2][k])

    def swap_half(x):
        return across(x, lambda c: tiles // 2)

    def turn(x, shift):
        return lax.ppermute(x, "cam", [(c, (c + shift) % cams) for c in range(cams)])

    steps = len(orders[0])
    shape = jax.ShapeDtypeStruct
    piece_rows = 2 * rows // cams
    where = jnp.stack((tile, cam)).astype(jnp.int32)
    lanes = -(-blocks // LANES) * LANES
    fixed = (keys, values, queries, grad_out, visible, counts.reshape(1, blocks))
    held, query_near, grad_near, message, table = run(
        functools.partial(start_kernel, cams),
        (
            shape((shard_rows, 2 * width), BF16),
            shape((rows, width), BF16),
            shape((rows, width), BF16),
            shape((piece_rows + 16, width), BF16),
            shape((LANES, lanes), BF16),
        ),
        (where, *(pltpu.with_memory_space_constraint(x, pltpu.HBM) for x in fixed)),
        scratch=(
            pltpu.VMEM(visible.shape, visible.dtype),
            pltpu.VMEM((1, blocks), counts.dtype),
            pltpu.SemaphoreType.DMA((len(fixed),)),
        ),
        smem=1,
        space=pltpu.HBM,
    )
    received = swap_half(message)
    for k in range(steps - 2):
        held = jnp.concatenate((held, step(held, k)), axis=0)
    nearer = step(held, steps - 2)
    farther = step(held, steps - 1)
    farthest = across(held, lambda c: orders[c % 2][-1] ^ orders[c % 2][-2])
    pieces = [received] + [turn(received, shift) for shift in range(1, cams)]
    held = jnp.concatenate((held, nearer), axis=0)
    last = jnp.concatenate((farther, farthest), axis=0)

    all_rows = 2 * rows
    chunk = held.shape[0]
    work = 2 * all_rows * chunk * width
    stats, query_t, grad_t, bias = run(
        functools.partial(first_kernel, cams, blocks, masks, shard_rows, block_keys, span, tile_rows, factor),
        (
            shape((3 * H, all_rows), F32),
            shape((width, all_rows), BF16),
            shape((width, all_rows), BF16),
            shape((2 * chunk, LANES), BF16),
        ),
        (where, query_near, grad_near, *pieces, held, table),
        scratch=(pltpu.VMEM((2 * rows, width), BF16), pltpu.VMEM((LANES, lanes), BF16)),
        smem=1,
        flops=8 * work,
    )
    (stats,) = run(
        functools.partial(second_kernel, span, tile_rows, factor),
        (shape((3 * H, all_rows), F32),),
        (last, bias, query_t, grad_t, stats),
        flops=8 * work,
    )
    near = combine([stats] + [turn(stats, shift) for shift in range(1, cams)], factor)
    opposite = swap_half(near)
    weights, dprobs = run(
        functools.partial(near_kernel, span, tile_rows, factor),
        (shape((chunk, H * all_rows), F32), shape((chunk, H * all_rows), F32)),
        (near, last, bias, query_t, grad_t),
        flops=8 * work,
    )

    scratch = (pltpu.VMEM((2 * width, chunk), F32),)
    sent, query_sum, ends = run(
        functools.partial(third_kernel, span, scale),
        (shape((chunk, 2 * width), BF16), shape((width, all_rows), F32), shape((2 * H, all_rows), F32)),
        (near, opposite, last, query_t, grad_t, weights, dprobs),
        scratch=(*scratch, pltpu.VMEM((H, all_rows), F32)),
        flops=20 * work,
    )
    got = step(sent, steps - 1)
    part = rows // cams
    kept, query_part, *to_turn = run(
        functools.partial(fourth_kernel, cams, span, tile_rows, factor, scale),
        (
            shape((chunk, 2 * width), F32),
            shape((2 * part, width), F32),
            *(shape((2 * part, width), BF16) for _ in range(1, cams)),
        ),
        (where, ends, query_sum, held, bias, query_t, grad_t),
        scratch=(pltpu.VMEM((width, all_rows), F32), *scratch, pltpu.VMEM((all_rows, width), F32)),
        smem=1,
        flops=20 * work,
    )
    for shift in range(1, cams):
        query_part = query_part + turn(to_turn[shift - 1], shift).astype(F32)
    query_far = query_part[part:].astype(BF16)
    query_got = swap_half(query_far)
    sums = kept + got.astype(F32)
    slots = [sums[k * shard_rows : (k + 1) * shard_rows] for k in range(chunk // shard_rows)]
    outs = [slot.astype(BF16) for slot in slots[1:]]
    owned = slots[0]
    for k, out in enumerate(outs):
        owned = owned + across(out, lambda c: masks[c % 2][k + 1]).astype(F32)
    owned = owned.astype(BF16)
    mine = (query_part[:part] + query_got.astype(F32)).astype(BF16)
    parts = [mine] + [turn(mine, shift) for shift in range(1, cams)]
    ordered = []
    for k in range(cams):
        source = (cam + cams - k) % cams
        ordered.append(functools.reduce(lambda x, s: jnp.where(source == s, parts[s], x), range(1, cams), parts[0]))
    query_part = jnp.concatenate(ordered, axis=0)
    return (query_part, owned[:, :width], owned[:, width:])


def solution(mesh):
    in_specs = (
        P("tile", None),
        P(("cam", "tile"), None),
        P(("cam", "tile"), None),
        P("tile", None),
        P("tile", "cam"),
        P("cam"),
    )
    out_specs = (P("tile", None), P(("cam", "tile"), None), P(("cam", "tile"), None))

    return jax.shard_map(shards, mesh=mesh, in_specs=in_specs, out_specs=out_specs, check_vma=False)
```

time: 50.6 us -> 54.8 us (1.083)
  starting transfers between devices: 10.9 us -> 21.8 us
  waiting for transfers between devices: 26 us -> 19 us
  Pallas kernels: 8.58 us -> 11.5 us
  local copies, waits for them, and re-layouts: 2.96 us -> 0.71 us
    ppermute x9 -> x11, starting transfers between devices: 10.7 us -> 21.6 us  [across(): return lax.ppermute(x, ('cam', 'tile'), pairs)]
    ppermute x9 -> x11, waiting for transfers between devices: 22.9 us -> 16.4 us  [across(): return lax.ppermute(x, ('cam', 'tile'), pairs)]
    pallas_call x4 -> x6, Pallas kernels: 8.58 us -> 11.5 us  [run(): pl.pallas_call(kernel, out_shape=tuple(outs), in_specs=[pl.BlockSpec(memo...]
    unnamed x9 -> x3, local copies, waits for them, and re-layouts: 1.49 us -> 0.03 us
    concatenate x2, local copies, waits for them, and re-layouts: 0.84 us -> 0.02 us  [the longest x1 0.01 us: shards(): last = jnp.concatenate((farther, farthest), axis=0)]
    convert_element_type x6 -> x2, other arithmetic: 0.84 us -> 0.05 us  [the longest x1 0.03 us: shards(): owned = owned.astype(BF16)]
    ppermute x3 -> x4, waiting for transfers between devices: 3.13 us -> 2.56 us  [turn(): lax.ppermute(x, 'cam', [(c, (c + shift) % cams) for c in range(cams)])]
  transfers between devices with their start and end apart: 12 -> 15, of which waited for: 9 -> 9; matrix products, arithmetic and copies ran while one was open for 2% -> 1% of each run, Pallas kernels for 9% -> 2%
where the time goes in v1:
time: 54.8 us; the launch traced here: 54.7 us
  starting transfers between devices  21.8 us (40%)
  waiting for transfers between devices  19 us (35%)
  Pallas kernels  11.5 us (21%)
  other arithmetic  0.94 us (2%)
  between operations  0.81 us (1%)
  local copies, waits for them, and re-layouts  0.71 us (1%)
    ppermute x11, starting transfers between devices, across(): return lax.ppermute(x, ('cam', 'tile'), pairs)  21.6 us
    ppermute x11, waiting for transfers between devices, across(): return lax.ppermute(x, ('cam', 'tile'), pairs)  16.4 us
    pallas_call x6, Pallas kernels, run(): pl.pallas_call(kernel, out_shape=tuple(outs), in_specs=[pl.BlockSpec(memo...  11.5 us
    ppermute x4, waiting for transfers between devices, turn(): lax.ppermute(x, 'cam', [(c, (c + shift) % cams) for c in range(cams)])  2.56 us
  transfers between devices with their start and end apart: 15, of which 9 were waited for; matrix products, arithmetic and copies ran while one was open for 1% of the time, Pallas kernels for 2%

profile of v1, /device:TPU:0, one launch (start us, length us, event | category | flops | bytes accessed | tf_op | source)
XLA Modules:
  0.0 54.7 jit_solution(12892241237951660301)
XLA Ops:
  0.6 0.1 pad_add_fusion.where_ref
  0.7 1.6 %shard_map.85 = (bf16[64,512]{1,0:T(8,128)(2,1)S(1)}, bf16[256,256]{1,0:T(8,128)(2,1)S(1)}, bf16[256,256]{1,0:T(8,128)(2,1)S(1)}, bf16[272,256]{1,0:T(8,128)(2,1)S(1)}, bf16[128,128]{1,0:T(8,128)(2,1)S(1)}) custom-call(s32[2]{0:T(128)S(1)} %pad_add_fusion.where_ref, bf16[64,256]{1,0:T(8,128)(2,1)} %key_ref.1, bf16[64,256]{1,0:T(8,128)(2,1)} %value_ref.1, ...), custom_call_target="tpu_custom_call" | custom-call | bytes 827784 | tf_op jit(solution)/shard_map/pallas_call | solution.py:304
  2.3 3.1 %collective-permute-start = (bf16[64,512]{1,0:T(8,128)(2,1)S(1)}, bf16[64,512]{1,0:T(8,128)(2,1)S(1)}, u32[]{:S(2)}, u32[]{:S(2)}) collective-permute-start(bf16[64,512]{1,0:T(8,128)(2,1)S(1)} %get-tuple-element.20), channel_id=1, source_target_pairs={{0,4},{1,5},{2,6},{3,7},{4,0},{5,1},{6,2},{7,3},{8,12},{9,13},{10,... | collective-permute-start | bytes 196616 | tf_op jit(solution)/shard_map/ppermute | solution.py:341
  5.4 2.6 %collective-permute-start.3 = (bf16[272,256]{1,0:T(8,128)(2,1)S(1)}, bf16[272,256]{1,0:T(8,128)(2,1)S(1)}, u32[]{:S(2)}, u32[]{:S(2)}) collective-permute-start(bf16[272,256]{1,0:T(8,128)(2,1)S(1)} %get-tuple-element.23), channel_id=1, source_target_pairs={{0,8},{1,9},{2,10},{3,11},{4,12},{5,13},{6,14},{7,15},{8,0},{9,1},... | collective-permute-start | bytes 417800 | tf_op jit(solution)/shard_map/ppermute | solution.py:341
  8.0 0.0 collective-permute-done
  8.1 1.6 %collective-permute-start.1 = (bf16[128,512]{1,0:T(8,128)(2,1)S(1)}, bf16[128,512]{1,0:T(8,128)(2,1)S(1)}, u32[]{:S(2)}, u32[]{:S(2)}) collective-permute-start(bf16[128,512]{1,0:T(8,128)(2,1)S(1)} %get-tuple-element.49), channel_id=1, source_target_pairs={{0,1},{1,0},{2,3},{3,2},{4,5},{5,4},{6,7},{7,6},{8,9},{9,8},{10,11... | collective-permute-start | bytes 393224 | tf_op jit(solution)/shard_map/ppermute | solution.py:341
  9.7 1.5 %collective-permute-start.5 = (bf16[128,512]{1,0:T(8,128)(2,1)S(1)}, bf16[128,512]{1,0:T(8,128)(2,1)S(1)}, u32[]{:S(2)}, u32[]{:S(2)}) collective-permute-start(bf16[128,512]{1,0:T(8,128)(2,1)S(1)} %get-tuple-element.49), channel_id=1, source_target_pairs={{0,2},{1,3},{2,0},{3,1},{4,6},{5,7},{6,4},{7,5},{8,10},{9,11},{10,... | collective-permute-start | bytes 393224 | tf_op jit(solution)/shard_map/ppermute | solution.py:341
  11.2 0.4 collective-permute-start.2
  11.6 2.8 %collective-permute-done.3.refs_0_ = bf16[272,256]{1,0:T(8,128)(2,1)S(1)} collective-permute-done((bf16[272,256]{1,0:T(8,128)(2,1)S(1)}, bf16[272,256]{1,0:T(8,128)(2,1)S(1)}, u32[]{:S(2)}, u32[]{:S(2)}) %collective-permute-start.3) | collective-permute-done | bytes 139296 | tf_op jit(solution)/shard_map/ppermute | solution.py:341
  14.4 0.0 collective-permute-start.4
  14.4 0.1 collective-permute-done.1
  14.5 3.0 %collective-permute-done.5 = bf16[128,512]{1,0:T(8,128)(2,1)S(1)} collective-permute-done((bf16[128,512]{1,0:T(8,128)(2,1)S(1)}, bf16[128,512]{1,0:T(8,128)(2,1)S(1)}, u32[]{:S(2)}, u32[]{:S(2)}) %collective-permute-start.5) | collective-permute-done | bytes 131104 | tf_op jit(solution)/shard_map/ppermute | solution.py:341
  17.5 0.0 collective-permute-done.2
  17.5 0.0 collective-permute-done.4.refs_1_
  17.5 2.2 %shard_map.86 = (f32[24,512]{1,0:T(8,128)S(1)}, bf16[256,512]{1,0:T(8,128)(2,1)S(1)}, bf16[256,512]{1,0:T(8,128)(2,1)S(1)}, bf16[512,128]{1,0:T(8,128)(2,1)S(1)}) custom-call(s32[2]{0:T(128)S(1)} %pad_add_fusion.where_ref, bf16[256,256]{1,0:T(8,128)(2,1)S(1)} %get-tuple-element.21.query_ref, bf16[256,256]{1,0:T(8,128)(2,1)S(1)} %get-tuple-element.22.grad_ref, ...), custom_call_target="tpu_custom_call" | custom-call | flops 536870912 | bytes 1540104 | tf_op jit(solution)/shard_map/pallas_call | solution.py:304
  19.7 1.6 %shard_map.87 = f32[24,512]{1,0:T(8,128)S(1)} custom-call(bf16[256,512]{1,0:T(8,128)(2,1)S(1)} %constant_dynamic-update-slice_fusion.2.chunk_ref, bf16[512,128]{1,0:T(8,128)(2,1)S(1)} %get-tuple-element.25.bias_ref, bf16[256,512]{1,0:T(8,128)(2,1)S(1)} %get-tuple-element.26.query_t_ref, bf16[256,512]{1,0:T(8,128)(2,1)S(1)} %get-tuple-element.27.grad_t_ref, ...), custom_call_target="tpu_custom_call" | custom-call | flops 536870912 | bytes 1015808 | tf_op jit(solution)/shard_map/pallas_call | solution.py:304
  21.2 0.1 collective-permute-start.6
  21.3 1.2 %collective-permute-done.6 = f32[24,512]{1,0:T(8,128)S(1)} collective-permute-done((f32[24,512]{1,0:T(8,128)S(1)}, f32[24,512]{1,0:T(8,128)S(1)}, u32[]{:S(2)}, u32[]{:S(2)}) %collective-permute-start.6) | collective-permute-done | bytes 49184 | tf_op jit(solution)/shard_map/ppermute | solution.py:350
  22.6 2.9 %collective-permute-start.7 = (f32[16,512]{1,0:T(8,128)S(1)}, f32[16,512]{1,0:T(8,128)S(1)}, u32[]{:S(2)}, u32[]{:S(2)}) collective-permute-start(f32[16,512]{1,0:T(8,128)S(1)} %pad_maximum_fusion.1.near_ref), channel_id=1, source_target_pairs={{0,8},{1,9},{2,10},{3,11},{4,12},{5,13},{6,14},{7,15},{8,0},{9,1},... | collective-permute-start | bytes 98312 | tf_op jit(solution)/shard_map/ppermute | solution.py:341
  25.5 1.2 %shard_map.88 = (f32[256,4096]{1,0:T(8,128)S(1)}, f32[256,4096]{1,0:T(8,128)S(1)}) custom-call(f32[16,512]{1,0:T(8,128)S(1)} %pad_maximum_fusion.1.near_ref, bf16[256,512]{1,0:T(8,128)(2,1)S(1)} %constant_dynamic-update-slice_fusion.2.chunk_ref, bf16[512,128]{1,0:T(8,128)(2,1)S(1)} %get-tuple-element.25.bias_ref, ...), custom_call_target="tpu_custom_call" | custom-call | flops 536870912 | bytes 9338880 | tf_op jit(solution)/shard_map/pallas_call | solution.py:304
  26.8 0.7 %collective-permute-done.7.across_ref = f32[16,512]{1,0:T(8,128)S(1)} collective-permute-done((f32[16,512]{1,0:T(8,128)S(1)}, f32[16,512]{1,0:T(8,128)S(1)}, u32[]{:S(2)}, u32[]{:S(2)}) %collective-permute-start.7) | collective-permute-done | bytes 32800 | tf_op jit(solution)/shard_map/ppermute | solution.py:341
  27.5 1.8 %shard_map.89 = (bf16[256,512]{1,0:T(8,128)(2,1)S(1)}, f32[256,512]{1,0:T(8,128)S(1)}, f32[16,512]{1,0:T(8,128)S(1)}) custom-call(f32[16,512]{1,0:T(8,128)S(1)} %pad_maximum_fusion.1.near_ref, f32[16,512]{1,0:T(8,128)S(1)} %collective-permute-done.7.across_ref, bf16[256,512]{1,0:T(8,128)(2,1)S(1)} %constant_dynamic-update-slice_fusion.2.chunk_ref, ...), custom_call_target="tpu_custom_call" | custom-call | flops 1342177280 | bytes 10059776 | tf_op jit(solution)/shard_map/pallas_call | solution.py:304
  29.3 3.1 %shard_map.90 = (f32[256,512]{1,0:T(8,128)S(1)}, f32[256,256]{1,0:T(8,128)S(1)}, bf16[256,256]{1,0:T(8,128)(2,1)S(1)}) custom-call(s32[2]{0:T(128)S(1)} %pad_add_fusion.where_ref, f32[16,512]{1,0:T(8,128)S(1)} %get-tuple-element.31.ends_ref, f32[256,512]{1,0:T(8,128)S(1)} %get-tuple-element.32.before_ref, ...), custom_call_target="tpu_custom_call" | custom-call | flops 1342177280 | bytes 2392072 | tf_op jit(solution)/shard_map/pallas_call | solution.py:304
  32.4 0.1 collective-permute-start.8
  32.5 1.3 %collective-permute-done.8 = bf16[256,256]{1,0:T(8,128)(2,1)S(1)} collective-permute-done((bf16[256,256]{1,0:T(8,128)(2,1)S(1)}, bf16[256,256]{1,0:T(8,128)(2,1)S(1)}, u32[]{:S(2)}, u32[]{:S(2)}) %collective-permute-start.8) | collective-permute-done | bytes 131104 | tf_op jit(solution)/shard_map/ppermute | solution.py:350
  33.9 2.9 %collective-permute-start.9 = (bf16[128,256]{1,0:T(8,128)(2,1)S(1)}, bf16[128,256]{1,0:T(8,128)(2,1)S(1)}, u32[]{:S(2)}, u32[]{:S(2)}) collective-permute-start(bf16[128,256]{1,0:T(8,128)(2,1)S(1)} %slice.133), channel_id=1, source_target_pairs={{0,8},{1,9},{2,10},{3,11},{4,12},{5,13},{6,14},{7,15},{8,0},{9,1},... | collective-permute-start | bytes 196616 | tf_op jit(solution)/shard_map/ppermute | solution.py:341
  36.8 2.4 %collective-permute-done.9 = bf16[128,256]{1,0:T(8,128)(2,1)S(1)} collective-permute-done((bf16[128,256]{1,0:T(8,128)(2,1)S(1)}, bf16[128,256]{1,0:T(8,128)(2,1)S(1)}, u32[]{:S(2)}, u32[]{:S(2)}) %collective-permute-start.9) | collective-permute-done | bytes 65568 | tf_op jit(solution)/shard_map/ppermute | solution.py:341
  39.2 0.1 collective-permute-start.10
  39.3 2.1 %collective-permute-start.11 = (bf16[256,512]{1,0:T(8,128)(2,1)S(1)}, bf16[256,512]{1,0:T(8,128)(2,1)S(1)}, u32[]{:S(2)}, u32[]{:S(2)}) collective-permute-start(bf16[256,512]{1,0:T(8,128)(2,1)S(1)} %get-tuple-element.36), channel_id=1, source_target_pairs={{0,1},{1,0},{2,3},{3,2},{4,5},{5,4},{6,7},{7,6},{8,9},{9,8},{10,11... | collective-permute-start | bytes 786440 | tf_op jit(solution)/shard_map/ppermute | solution.py:341
  41.5 0.0 collective-permute-done.10
  41.5 4.3 %collective-permute-done.11 = bf16[256,512]{1,0:T(8,128)(2,1)S(1)} collective-permute-done((bf16[256,512]{1,0:T(8,128)(2,1)S(1)}, bf16[256,512]{1,0:T(8,128)(2,1)S(1)}, u32[]{:S(2)}, u32[]{:S(2)}) %collective-permute-start.11) | collective-permute-done | bytes 262176 | tf_op jit(solution)/shard_map/ppermute | solution.py:341
  45.8 0.1 fusion.7
  45.9 2.1 %collective-permute-start.12 = (bf16[64,512]{1,0:T(8,128)(2,1)S(1)}, bf16[64,512]{1,0:T(8,128)(2,1)S(1)}, u32[]{:S(2)}, u32[]{:S(2)}) collective-permute-start(bf16[64,512]{1,0:T(8,128)(2,1)S(1)} %get-tuple-element.39), channel_id=1, source_target_pairs={{0,4},{1,5},{2,6},{3,7},{4,0},{5,1},{6,2},{7,3},{8,12},{9,13},{10,... | collective-permute-start | bytes 196616 | tf_op jit(solution)/shard_map/ppermute | solution.py:341
  48.1 0.8 %collective-permute-start.13 = (bf16[64,512]{1,0:T(8,128)(2,1)S(1)}, bf16[64,512]{1,0:T(8,128)(2,1)S(1)}, u32[]{:S(2)}, u32[]{:S(2)}) collective-permute-start(bf16[64,512]{1,0:T(8,128)(2,1)S(1)} %get-tuple-element.41), channel_id=1, source_target_pairs={{0,2},{1,3},{2,0},{3,1},{4,6},{5,7},{6,4},{7,5},{8,10},{9,11},{10,... | collective-permute-start | bytes 196616 | tf_op jit(solution)/shard_map/ppermute | solution.py:341
  48.9 1.3 %collective-permute-start.14 = (bf16[64,512]{1,0:T(8,128)(2,1)S(1)}, bf16[64,512]{1,0:T(8,128)(2,1)S(1)}, u32[]{:S(2)}, u32[]{:S(2)}) collective-permute-start(bf16[64,512]{1,0:T(8,128)(2,1)S(1)} %get-tuple-element.40), channel_id=1, source_target_pairs={{0,6},{1,7},{2,4},{3,5},{4,2},{5,3},{6,0},{7,1},{8,14},{9,15},{10,... | collective-permute-start | bytes 196616 | tf_op jit(solution)/shard_map/ppermute | solution.py:341
  50.2 0.7 %pad_maximum_fusion = bf16[256,256]{1,0:T(8,128)(2,1)} fusion(bf16[128,256]{1,0:T(8,128)(2,1)S(1)} %get-tuple-element.43, bf16[128,256]{1,0:T(8,128)(2,1)S(1)} %get-tuple-element.42), kind=kLoop, calls=%fused_computation.9 | loop fusion | flops 262144 | bytes 262144 | tf_op jit(solution)/shard_map/concatenate | solution.py:456
  50.9 0.0 collective-permute-done.12
  50.9 1.4 %collective-permute-done.13 = bf16[64,512]{1,0:T(8,128)(2,1)S(1)} collective-permute-done((bf16[64,512]{1,0:T(8,128)(2,1)S(1)}, bf16[64,512]{1,0:T(8,128)(2,1)S(1)}, u32[]{:S(2)}, u32[]{:S(2)}) %collective-permute-start.13) | collective-permute-done | bytes 65568 | tf_op jit(solution)/shard_map/ppermute | solution.py:341
  52.3 1.7 %collective-permute-done.14 = bf16[64,512]{1,0:T(8,128)(2,1)S(1)} collective-permute-done((bf16[64,512]{1,0:T(8,128)(2,1)S(1)}, bf16[64,512]{1,0:T(8,128)(2,1)S(1)}, u32[]{:S(2)}, u32[]{:S(2)}) %collective-permute-start.14) | collective-permute-done | bytes 65568 | tf_op jit(solution)/shard_map/ppermute | solution.py:341
  54.1 0.6 %fusion.9 = (bf16[64,256]{1,0:T(8,128)(2,1)}, bf16[64,256]{1,0:T(8,128)(2,1)}) fusion(bf16[64,512]{1,0:T(8,128)(2,1)S(1)} %fusion.2), kind=kLoop, calls=%fused_computation.34 | loop fusion | bytes 131072 | tf_op jit(solution)/shard_map/slice | solution.py:457
  (13 shorter events, 0.2 us)
Async XLA Ops:
  2.3 5.7 %collective-permute-start = (bf16[64,512]{1,0:T(8,128)(2,1)S(1)}, bf16[64,512]{1,0:T(8,128)(2,1)S(1)}, u32[]{:S(2)}, u32[]{:S(2)}) collective-permute-start(bf16[64,512]{1,0:T(8,128)(2,1)S(1)} %get-tuple-element.20), channel_id=1, source_target_pairs={{0,4},{1,5},{2,6},{3,7},{4,0},{5,1},{6,2},{7,3},{8,12},{9,13},{10,... | collective-permute-start | bytes 196616 | tf_op jit(solution)/shard_map/ppermute | solution.py:341
  5.4 9.0 %collective-permute-start.3 = (bf16[272,256]{1,0:T(8,128)(2,1)S(1)}, bf16[272,256]{1,0:T(8,128)(2,1)S(1)}, u32[]{:S(2)}, u32[]{:S(2)}) collective-permute-start(bf16[272,256]{1,0:T(8,128)(2,1)S(1)} %get-tuple-element.23), channel_id=1, source_target_pairs={{0,8},{1,9},{2,10},{3,11},{4,12},{5,13},{6,14},{7,15},{8,0},{9,1},... | collective-permute-start | bytes 417800 | tf_op jit(solution)/shard_map/ppermute | solution.py:341
  8.1 6.4 %collective-permute-start.1 = (bf16[128,512]{1,0:T(8,128)(2,1)S(1)}, bf16[128,512]{1,0:T(8,128)(2,1)S(1)}, u32[]{:S(2)}, u32[]{:S(2)}) collective-permute-start(bf16[128,512]{1,0:T(8,128)(2,1)S(1)} %get-tuple-element.49), channel_id=1, source_target_pairs={{0,1},{1,0},{2,3},{3,2},{4,5},{5,4},{6,7},{7,6},{8,9},{9,8},{10,11... | collective-permute-start | bytes 393224 | tf_op jit(solution)/shard_map/ppermute | solution.py:341
  9.7 7.8 %collective-permute-start.5 = (bf16[128,512]{1,0:T(8,128)(2,1)S(1)}, bf16[128,512]{1,0:T(8,128)(2,1)S(1)}, u32[]{:S(2)}, u32[]{:S(2)}) collective-permute-start(bf16[128,512]{1,0:T(8,128)(2,1)S(1)} %get-tuple-element.49), channel_id=1, source_target_pairs={{0,2},{1,3},{2,0},{3,1},{4,6},{5,7},{6,4},{7,5},{8,10},{9,11},{10,... | collective-permute-start | bytes 393224 | tf_op jit(solution)/shard_map/ppermute | solution.py:341
  11.2 6.3 %collective-permute-start.2 = (bf16[128,512]{1,0:T(8,128)(2,1)S(1)}, bf16[128,512]{1,0:T(8,128)(2,1)S(1)}, u32[]{:S(2)}, u32[]{:S(2)}) collective-permute-start(bf16[128,512]{1,0:T(8,128)(2,1)S(1)} %get-tuple-element.49), channel_id=1, source_target_pairs={{0,3},{1,2},{2,1},{3,0},{4,7},{5,6},{6,5},{7,4},{8,11},{9,10},{10,... | collective-permute-start | bytes 393224 | tf_op jit(solution)/shard_map/ppermute | solution.py:341
  14.4 3.1 %collective-permute-start.4 = (bf16[272,256]{1,0:T(8,128)(2,1)S(1)}, bf16[272,256]{1,0:T(8,128)(2,1)S(1)}, u32[]{:S(2)}, u32[]{:S(2)}) collective-permute-start(bf16[272,256]{1,0:T(8,128)(2,1)S(1)} %collective-permute-done.3.refs_0_), channel_id=1, source_target_pairs={{0,16},{16,0},{1,17},{17,1},{2,18},{18,2},{3,19},{19,3},{4,20},{20... | collective-permute-start | bytes 417800 | tf_op jit(solution)/shard_map/ppermute | solution.py:350
  21.2 1.3 %collective-permute-start.6 = (f32[24,512]{1,0:T(8,128)S(1)}, f32[24,512]{1,0:T(8,128)S(1)}, u32[]{:S(2)}, u32[]{:S(2)}) collective-permute-start(f32[24,512]{1,0:T(8,128)S(1)} %shard_map.87), channel_id=1, source_target_pairs={{0,16},{16,0},{1,17},{17,1},{2,18},{18,2},{3,19},{19,3},{4,20},{20... | collective-permute-start | bytes 147464 | tf_op jit(solution)/shard_map/ppermute | solution.py:350
  22.6 4.9 %collective-permute-start.7 = (f32[16,512]{1,0:T(8,128)S(1)}, f32[16,512]{1,0:T(8,128)S(1)}, u32[]{:S(2)}, u32[]{:S(2)}) collective-permute-start(f32[16,512]{1,0:T(8,128)S(1)} %pad_maximum_fusion.1.near_ref), channel_id=1, source_target_pairs={{0,8},{1,9},{2,10},{3,11},{4,12},{5,13},{6,14},{7,15},{8,0},{9,1},... | collective-permute-start | bytes 98312 | tf_op jit(solution)/shard_map/ppermute | solution.py:341
  32.4 1.4 %collective-permute-start.8 = (bf16[256,256]{1,0:T(8,128)(2,1)S(1)}, bf16[256,256]{1,0:T(8,128)(2,1)S(1)}, u32[]{:S(2)}, u32[]{:S(2)}) collective-permute-start(bf16[256,256]{1,0:T(8,128)(2,1)S(1)} %get-tuple-element.34), channel_id=1, source_target_pairs={{0,16},{16,0},{1,17},{17,1},{2,18},{18,2},{3,19},{19,3},{4,20},{20... | collective-permute-start | bytes 393224 | tf_op jit(solution)/shard_map/ppermute | solution.py:350
  33.9 5.4 %collective-permute-start.9 = (bf16[128,256]{1,0:T(8,128)(2,1)S(1)}, bf16[128,256]{1,0:T(8,128)(2,1)S(1)}, u32[]{:S(2)}, u32[]{:S(2)}) collective-permute-start(bf16[128,256]{1,0:T(8,128)(2,1)S(1)} %slice.133), channel_id=1, source_target_pairs={{0,8},{1,9},{2,10},{3,11},{4,12},{5,13},{6,14},{7,15},{8,0},{9,1},... | collective-permute-start | bytes 196616 | tf_op jit(solution)/shard_map/ppermute | solution.py:341
  39.2 2.2 %collective-permute-start.10 = (bf16[128,256]{1,0:T(8,128)(2,1)S(1)}, bf16[128,256]{1,0:T(8,128)(2,1)S(1)}, u32[]{:S(2)}, u32[]{:S(2)}) collective-permute-start(bf16[128,256]{1,0:T(8,128)(2,1)S(1)} %fusion.3), channel_id=1, source_target_pairs={{0,16},{16,0},{1,17},{17,1},{2,18},{18,2},{3,19},{19,3},{4,20},{20... | collective-permute-start | bytes 196616 | tf_op jit(solution)/shard_map/ppermute | solution.py:350
  39.3 6.5 %collective-permute-start.11 = (bf16[256,512]{1,0:T(8,128)(2,1)S(1)}, bf16[256,512]{1,0:T(8,128)(2,1)S(1)}, u32[]{:S(2)}, u32[]{:S(2)}) collective-permute-start(bf16[256,512]{1,0:T(8,128)(2,1)S(1)} %get-tuple-element.36), channel_id=1, source_target_pairs={{0,1},{1,0},{2,3},{3,2},{4,5},{5,4},{6,7},{7,6},{8,9},{9,8},{10,11... | collective-permute-start | bytes 786440 | tf_op jit(solution)/shard_map/ppermute | solution.py:341
  45.9 5.0 %collective-permute-start.12 = (bf16[64,512]{1,0:T(8,128)(2,1)S(1)}, bf16[64,512]{1,0:T(8,128)(2,1)S(1)}, u32[]{:S(2)}, u32[]{:S(2)}) collective-permute-start(bf16[64,512]{1,0:T(8,128)(2,1)S(1)} %get-tuple-element.39), channel_id=1, source_target_pairs={{0,4},{1,5},{2,6},{3,7},{4,0},{5,1},{6,2},{7,3},{8,12},{9,13},{10,... | collective-permute-start | bytes 196616 | tf_op jit(solution)/shard_map/ppermute | solution.py:341
  48.1 4.3 %collective-permute-start.13 = (bf16[64,512]{1,0:T(8,128)(2,1)S(1)}, bf16[64,512]{1,0:T(8,128)(2,1)S(1)}, u32[]{:S(2)}, u32[]{:S(2)}) collective-permute-start(bf16[64,512]{1,0:T(8,128)(2,1)S(1)} %get-tuple-element.41), channel_id=1, source_target_pairs={{0,2},{1,3},{2,0},{3,1},{4,6},{5,7},{6,4},{7,5},{8,10},{9,11},{10,... | collective-permute-start | bytes 196616 | tf_op jit(solution)/shard_map/ppermute | solution.py:341
  48.9 5.2 %collective-permute-start.14 = (bf16[64,512]{1,0:T(8,128)(2,1)S(1)}, bf16[64,512]{1,0:T(8,128)(2,1)S(1)}, u32[]{:S(2)}, u32[]{:S(2)}) collective-permute-start(bf16[64,512]{1,0:T(8,128)(2,1)S(1)} %get-tuple-element.40), channel_id=1, source_target_pairs={{0,6},{1,7},{2,4},{3,5},{4,2},{5,3},{6,0},{7,1},{8,14},{9,15},{10,... | collective-permute-start | bytes 196616 | tf_op jit(solution)/shard_map/ppermute | solution.py:341

commit v2 on v1

--- a/solution.py
+++ b/solution.py
@@ -30,7 +30,7 @@
     while bit < tiles // 2:
         bits.append(bit)
         bit *= 2
-    return (tuple(bits[::-1]), tuple(bits[:1:-1] + bits[:2]))
+    return (tuple(bits[:1] + bits[:0:-1]), tuple(bits[::-1]))
 
 
 def slot_masks(order):
@@ -40,7 +40,7 @@
     return masks
 
 
-def start_kernel(cams, where_ref, key_ref, value_ref, query_ref, grad_ref, seen_ref, limit_ref, pair_ref, query_out,
+def start_kernel(cams, key_ref, value_ref, query_ref, grad_ref, seen_ref, limit_ref, pair_ref, query_out,
                  grad_out, message_ref, table_ref, seen_vmem, limit_vmem, sems):
     rows, width = query_ref.shape
     own_tiles, blocks = seen_ref.shape
@@ -62,7 +62,7 @@
         copy.wait()
     for piece in range(cams):
 
-        @pl.when(where_ref[1] == piece)
+        @pl.when(lax.axis_index("cam") == piece)
         def _(first=piece * piece_rows):
             source, at = (query_out, first) if first < rows else (grad_out, first - rows)
             message_ref[:piece_rows, :] = source[at : at + piece_rows, :]
@@ -73,8 +73,8 @@
     table_ref[LANES - 1 : LANES, :blocks] = limit_vmem[...].astype(F32).astype(BF16)
 
 
-def build_bias(where_ref, table_ref, bias_ref, masks, shard_rows, block_keys):
-    tile, cam = where_ref[0], where_ref[1]
+def build_bias(table_ref, bias_ref, masks, shard_rows, block_keys):
+    tile, cam = lax.axis_index("tile"), lax.axis_index("cam")
     per_shard = shard_rows // block_keys
     lanes = table_ref.shape[1]
     table = table_ref[...]
@@ -142,7 +142,7 @@
             stats_ref[2 * H + head : 2 * H + head + 1, columns] = product
 
 
-def first_kernel(cams, blocks, masks, shard_rows, block_keys, span, tile_rows, factor, where_ref, query_ref, grad_ref, *refs):
+def first_kernel(cams, blocks, masks, shard_rows, block_keys, span, tile_rows, factor, query_ref, grad_ref, *refs):
     pieces, (chunk_ref, table_ref), outs = refs[:cams], refs[cams : cams + 2], refs[cams + 2 :]
     stats_ref, query_t_ref, grad_t_ref, bias_ref, far_ref, full_table_ref = outs
     rows, _ = query_ref.shape
@@ -150,10 +150,10 @@
     note = slice(2 * rows // cams, 2 * rows // cams + own_tiles)
     full_table_ref[...] = table_ref[...]
     full_table_ref[own_tiles : 2 * own_tiles, :blocks] = pieces[0][note, :blocks]
-    build_bias(where_ref, full_table_ref, bias_ref, masks, shard_rows, block_keys)
+    build_bias(full_table_ref, bias_ref, masks, shard_rows, block_keys)
     piece_rows = 2 * rows // cams
     for shift in range(cams):
-        piece = lax.rem(where_ref[1] + cams - shift, cams)
+        piece = lax.rem(lax.axis_index("cam") + cams - shift, cams)
         start = pl.multiple_of(piece * piece_rows, 16)
         far_ref[pl.ds(start, piece_rows), :] = pieces[shift][:piece_rows, :]
     query_t_ref[:, :rows] = query_ref[...].T
@@ -210,9 +210,9 @@
     staggered(len(blocks), (terms, store), (0, 1))
 
 
-def products_of(blocks, queries, query_t_ref, grad_t_ref, keys_t, query_sum_ref, before_ref, sums_ref, scale):
+def products_of(blocks, queries, query_t_ref, grad_t_ref, keys_t, query_sum_ref, before_ref, out_ref, scale):
     width = query_t_ref.shape[0]
-    partial = {}
+    partial, done = {}, {}
 
     def products(n, ready):
         head, columns = blocks[n]
@@ -230,14 +230,20 @@
         if columns.stop < queries:
             partial[head] = (key_part, value_part)
         else:
-            sums_ref[rows, :] = key_part * scale
-            sums_ref[width + rows.start : width + rows.stop, :] = value_part
+            done[head] = (key_part * scale, value_part)
+        if rows.stop % LANES == 0 and head in done:
+            heads = sorted(done)
+            for side in range(2):
+                group = jnp.concatenate([done[h][side] for h in heads], axis=0)
+                place = side * width + rows.stop - LANES
+                out_ref[:, place : place + LANES] = group.T.astype(out_ref.dtype)
+            done.clear()
 
     return products
 
 
 def third_kernel(span, scale, near_ref, across_ref, chunk_ref, query_t_ref, grad_t_ref, weights_ref, dprobs_ref,
-                 out_ref, query_sum_ref, ends_ref, sums_ref, shrink_ref):
+                 out_ref, query_sum_ref, ends_ref, shrink_ref):
     width, queries = query_t_ref.shape
     rows = queries // 2
     turned = jnp.concatenate((across_ref[:, rows:], across_ref[:, :rows]), axis=1)
@@ -258,14 +264,13 @@
         dscores = probs * (dprobs_ref[:, place] - ends_ref[H + head : H + head + 1, columns])
         return probs.astype(BF16), dscores.astype(BF16)
 
-    products = products_of(blocks, queries, query_t_ref, grad_t_ref, keys_t, query_sum_ref, None, sums_ref, scale)
+    products = products_of(blocks, queries, query_t_ref, grad_t_ref, keys_t, query_sum_ref, None, out_ref, scale)
     staggered(len(blocks), (rounded, products), (0, 1))
-    out_ref[...] = sums_ref[...].T.astype(out_ref.dtype)
-
-
-def fourth_kernel(cams, span, tile_rows, factor, scale, where_ref, ends_ref, before_ref, chunk_ref, bias_ref, query_t_ref,
+
+
+def fourth_kernel(cams, span, tile_rows, factor, scale, ends_ref, before_ref, chunk_ref, bias_ref, query_t_ref,
                   grad_t_ref, out_ref, keep_ref, *refs):
-    turn_refs, (query_sum_ref, sums_ref, whole_ref) = refs[: cams - 1], refs[cams - 1 :]
+    turn_refs, (query_sum_ref, whole_ref) = refs[: cams - 1], refs[cams - 1 :]
     width, queries = query_t_ref.shape
     keys, values = chunk_of(chunk_ref, width)
     keys_t = chunk_ref[:, :width].T
@@ -285,26 +290,30 @@
         dscores = probs * (raw[1] - ends_ref[H + head : H + head + 1, columns])
         return probs.astype(BF16), dscores.astype(BF16)
 
-    products = products_of(blocks, queries, query_t_ref, grad_t_ref, keys_t, query_sum_ref, before_ref, sums_ref, scale)
+    products = products_of(blocks, queries, query_t_ref, grad_t_ref, keys_t, query_sum_ref, before_ref, out_ref, scale)
     staggered(len(blocks), (terms, rounded, products), (0, 1, 2))
-    out_ref[...] = sums_ref[...].T.astype(out_ref.dtype)
-    whole_ref[...] = query_sum_ref[...].T * scale
     count = keep_ref.shape[0] // 2
+    if count % LANES:
+        whole_ref[...] = query_sum_ref[...].T
     for shift, ref in enumerate((keep_ref, *turn_refs)):
-        piece = lax.rem(where_ref[1] + shift, cams)
+        piece = lax.rem(lax.axis_index("cam") + shift, cams)
         for side in range(2):
-            start = pl.multiple_of(side * (queries // 2) + piece * count, 16)
-            ref[side * count : (side + 1) * count, :] = whole_ref[pl.ds(start, count), :].astype(ref.dtype)
-
-
-def run(kernel, outs, args, scratch=(), smem=0, flops=0, space=pltpu.VMEM):
+            start = pl.multiple_of(side * (queries // 2) + piece * count, count)
+            if count % LANES:
+                part = whole_ref[pl.ds(start, count), :]
+            else:
+                part = query_sum_ref[:, pl.ds(start, count)].T
+            ref[side * count : (side + 1) * count, :] = (part * scale).astype(ref.dtype)
+
+
+def run(kernel, outs, args, scratch=(), flops=0, space=pltpu.VMEM):
     size = lambda a: math.prod(a.shape) * a.dtype.itemsize
     moved = sum(size(a) for a in args) + sum(size(a) for a in outs)
     vmem = pl.BlockSpec(memory_space=pltpu.VMEM)
     return pl.pallas_call(
         kernel,
         out_shape=tuple(outs),
-        in_specs=[pl.BlockSpec(memory_space=pltpu.SMEM)] * smem + [pl.BlockSpec(memory_space=space)] * (len(args) - smem),
+        in_specs=[pl.BlockSpec(memory_space=space)] * len(args),
         out_specs=tuple([vmem] * len(outs)),
         scratch_shapes=list(scratch),
         cost_estimate=pl.CostEstimate(flops=flops, bytes_accessed=moved, transcendentals=flops // 64),
@@ -327,7 +336,7 @@
     scale = 1.0 / math.sqrt(head_dim)
     factor = scale * math.log2(math.e)
     tiles, cams = lax.axis_size("tile"), lax.axis_size("cam")
-    tile, cam = lax.axis_index("tile"), lax.axis_index("cam")
+    cam = lax.axis_index("cam")
     blocks = counts.shape[0]
     block_keys = shard_rows * tiles // blocks
     own_tiles = visible.shape[0]
@@ -352,7 +361,6 @@
     steps = len(orders[0])
     shape = jax.ShapeDtypeStruct
     piece_rows = 2 * rows // cams
-    where = jnp.stack((tile, cam)).astype(jnp.int32)
     lanes = -(-blocks // LANES) * LANES
     fixed = (keys, values, queries, grad_out, visible, counts.reshape(1, blocks))
     held, query_near, grad_near, message, table = run(
@@ -364,13 +372,12 @@
             shape((piece_rows + 16, width), BF16),
             shape((LANES, lanes), BF16),
         ),
-        (where, *(pltpu.with_memory_space_constraint(x, pltpu.HBM) for x in fixed)),
+        tuple(pltpu.with_memory_space_constraint(x, pltpu.HBM) for x in fixed),
         scratch=(
             pltpu.VMEM(visible.shape, visible.dtype),
             pltpu.VMEM((1, blocks), counts.dtype),
             pltpu.SemaphoreType.DMA((len(fixed),)),
         ),
-        smem=1,
         space=pltpu.HBM,
     )
     received = swap_half(message)
@@ -394,10 +401,9 @@
             shape((width, all_rows), BF16),
             shape((2 * chunk, LANES), BF16),
         ),
-        (where, query_near, grad_near, *pieces, held, table),
+        (query_near, grad_near, *pieces, held, table),
         scratch=(pltpu.VMEM((2 * rows, width), BF16), pltpu.VMEM((LANES, lanes), BF16)),
-        smem=1,
-        flops=8 * work,
+            flops=8 * work,
     )
     (stats,) = run(
         functools.partial(second_kernel, span, tile_rows, factor),
@@ -414,12 +420,11 @@
         flops=8 * work,
     )
 
-    scratch = (pltpu.VMEM((2 * width, chunk), F32),)
     sent, query_sum, ends = run(
         functools.partial(third_kernel, span, scale),
         (shape((chunk, 2 * width), BF16), shape((width, all_rows), F32), shape((2 * H, all_rows), F32)),
         (near, opposite, last, query_t, grad_t, weights, dprobs),
-        scratch=(*scratch, pltpu.VMEM((H, all_rows), F32)),
+        scratch=(pltpu.VMEM((H, all_rows), F32),),
         flops=20 * work,
     )
     got = step(sent, steps - 1)
@@ -431,10 +436,9 @@
             shape((2 * part, width), F32),
             *(shape((2 * part, width), BF16) for _ in range(1, cams)),
         ),
-        (where, ends, query_sum, held, bias, query_t, grad_t),
-        scratch=(pltpu.VMEM((width, all_rows), F32), *scratch, pltpu.VMEM((all_rows, width), F32)),
-        smem=1,
-        flops=20 * work,
+        (ends, query_sum, held, bias, query_t, grad_t),
+        scratch=(pltpu.VMEM((width, all_rows), F32), pltpu.VMEM((all_rows, width), F32)),
+            flops=20 * work,
     )
     for shift in range(1, cams):
         query_part = query_part + turn(to_turn[shift - 1], shift).astype(F32)
@@ -444,8 +448,8 @@
     slots = [sums[k * shard_rows : (k + 1) * shard_rows] for k in range(chunk // shard_rows)]
     outs = [slot.astype(BF16) for slot in slots[1:]]
     owned = slots[0]
-    for k, out in enumerate(outs):
-        owned = owned + across(out, lambda c: masks[c % 2][k + 1]).astype(F32)
+    for k in range(len(outs), 0, -1):
+        owned = owned + across(outs[k - 1], lambda c: masks[c % 2][k]).astype(F32)
     owned = owned.astype(BF16)
     mine = (query_part[:part] + query_got.astype(F32)).astype(BF16)
     parts = [mine] + [turn(mine, shift) for shift in range(1, cams)]

time: 54.8 us -> 54.1 us (0.987)
  waiting for transfers between devices: 19 us -> 24.6 us
  starting transfers between devices: 21.8 us -> 17.2 us
  Pallas kernels: 11.5 us -> 9.72 us
    ppermute x11, waiting for transfers between devices: 16.4 us -> 21.7 us  [across(): return lax.ppermute(x, ('cam', 'tile'), pairs)]
    ppermute x11, starting transfers between devices: 21.6 us -> 17 us  [across(): return lax.ppermute(x, ('cam', 'tile'), pairs)]
    pallas_call x6, Pallas kernels: 11.5 us -> 9.72 us  [run(): pl.pallas_call(kernel, out_shape=tuple(outs), in_specs=[pl.BlockSpec(memo...]
  transfers between devices with their start and end apart: 15 -> 15, of which waited for: 9 -> 13; matrix products, arithmetic and copies ran while one was open for 1% -> 1% of each run, Pallas kernels for 2% -> 2%
where the time goes in v2:
time: 54.1 us; the launch traced here: 53.9 us
  waiting for transfers between devices  24.6 us (45%)
  starting transfers between devices  17.2 us (32%)
  Pallas kernels  9.72 us (18%)
  other arithmetic  0.86 us (2%)
  between operations  0.8 us (1%)
  local copies, waits for them, and re-layouts  0.7 us (1%)
    ppermute x11, waiting for transfers between devices, across(): return lax.ppermute(x, ('cam', 'tile'), pairs)  21.7 us
    ppermute x11, starting transfers between devices, across(): return lax.ppermute(x, ('cam', 'tile'), pairs)  17 us
    pallas_call x6, Pallas kernels, run(): pl.pallas_call(kernel, out_shape=tuple(outs), in_specs=[pl.BlockSpec(memo...  9.72 us
    ppermute x4, waiting for transfers between devices, turn(): lax.ppermute(x, 'cam', [(c, (c + shift) % cams) for c in range(cams)])  2.91 us
  transfers between devices with their start and end apart: 15, of which 13 were waited for; matrix products, arithmetic and copies ran while one was open for 1% of the time, Pallas kernels for 2%

profile of v2, /device:TPU:0, one launch (start us, length us, event | category | flops | bytes accessed | tf_op | source)
XLA Modules:
  0.0 53.9 jit_solution(8289599771615822131)
XLA Ops:
  0.6 1.0 %shard_map.85 = (bf16[64,512]{1,0:T(8,128)(2,1)S(1)}, bf16[256,256]{1,0:T(8,128)(2,1)S(1)}, bf16[256,256]{1,0:T(8,128)(2,1)S(1)}, bf16[272,256]{1,0:T(8,128)(2,1)S(1)}, bf16[128,128]{1,0:T(8,128)(2,1)S(1)}) custom-call(bf16[64,256]{1,0:T(8,128)(2,1)} %key_ref.1, bf16[64,256]{1,0:T(8,128)(2,1)} %value_ref.1, bf16[256,256]{1,0:T(8,128)(2,1)} %query_ref.1, ...), custom_call_target="tpu_custom_call" | custom-call | bytes 827776 | tf_op jit(solution)/shard_map/pallas_call | solution.py:313
  1.7 3.0 %collective-permute-start = (bf16[64,512]{1,0:T(8,128)(2,1)S(1)}, bf16[64,512]{1,0:T(8,128)(2,1)S(1)}, u32[]{:S(2)}, u32[]{:S(2)}) collective-permute-start(bf16[64,512]{1,0:T(8,128)(2,1)S(1)} %get-tuple-element.20), channel_id=1, source_target_pairs={{0,1},{1,0},{2,3},{3,2},{4,5},{5,4},{6,7},{7,6},{8,9},{9,8},{10,11... | collective-permute-start | bytes 196616 | tf_op jit(solution)/shard_map/ppermute | solution.py:350
  4.7 2.6 %collective-permute-start.3 = (bf16[272,256]{1,0:T(8,128)(2,1)S(1)}, bf16[272,256]{1,0:T(8,128)(2,1)S(1)}, u32[]{:S(2)}, u32[]{:S(2)}) collective-permute-start(bf16[272,256]{1,0:T(8,128)(2,1)S(1)} %get-tuple-element.23), channel_id=1, source_target_pairs={{0,8},{1,9},{2,10},{3,11},{4,12},{5,13},{6,14},{7,15},{8,0},{9,1},... | collective-permute-start | bytes 417800 | tf_op jit(solution)/shard_map/ppermute | solution.py:350
  7.3 0.0 collective-permute-done
  7.3 1.7 %collective-permute-start.1 = (bf16[128,512]{1,0:T(8,128)(2,1)S(1)}, bf16[128,512]{1,0:T(8,128)(2,1)S(1)}, u32[]{:S(2)}, u32[]{:S(2)}) collective-permute-start(bf16[128,512]{1,0:T(8,128)(2,1)S(1)} %get-tuple-element.49), channel_id=1, source_target_pairs={{0,2},{1,3},{2,0},{3,1},{4,6},{5,7},{6,4},{7,5},{8,10},{9,11},{10,... | collective-permute-start | bytes 393224 | tf_op jit(solution)/shard_map/ppermute | solution.py:350
  9.1 1.6 %collective-permute-start.5 = (bf16[128,512]{1,0:T(8,128)(2,1)S(1)}, bf16[128,512]{1,0:T(8,128)(2,1)S(1)}, u32[]{:S(2)}, u32[]{:S(2)}) collective-permute-start(bf16[128,512]{1,0:T(8,128)(2,1)S(1)} %get-tuple-element.49), channel_id=1, source_target_pairs={{0,4},{1,5},{2,6},{3,7},{4,0},{5,1},{6,2},{7,3},{8,12},{9,13},{10,... | collective-permute-start | bytes 393224 | tf_op jit(solution)/shard_map/ppermute | solution.py:350
  10.7 0.2 collective-permute-start.2
  10.9 3.0 %collective-permute-done.3.refs_0_ = bf16[272,256]{1,0:T(8,128)(2,1)S(1)} collective-permute-done((bf16[272,256]{1,0:T(8,128)(2,1)S(1)}, bf16[272,256]{1,0:T(8,128)(2,1)S(1)}, u32[]{:S(2)}, u32[]{:S(2)}) %collective-permute-start.3) | collective-permute-done | bytes 139296 | tf_op jit(solution)/shard_map/ppermute | solution.py:350
  13.9 0.0 collective-permute-start.4
  13.9 0.9 %collective-permute-done.1 = bf16[128,512]{1,0:T(8,128)(2,1)S(1)} collective-permute-done((bf16[128,512]{1,0:T(8,128)(2,1)S(1)}, bf16[128,512]{1,0:T(8,128)(2,1)S(1)}, u32[]{:S(2)}, u32[]{:S(2)}) %collective-permute-start.1) | collective-permute-done | bytes 131104 | tf_op jit(solution)/shard_map/ppermute | solution.py:350
  14.8 0.4 collective-permute-done.5
  15.2 2.1 %collective-permute-done.2 = bf16[128,512]{1,0:T(8,128)(2,1)S(1)} collective-permute-done((bf16[128,512]{1,0:T(8,128)(2,1)S(1)}, bf16[128,512]{1,0:T(8,128)(2,1)S(1)}, u32[]{:S(2)}, u32[]{:S(2)}) %collective-permute-start.2) | collective-permute-done | bytes 131104 | tf_op jit(solution)/shard_map/ppermute | solution.py:350
  17.4 0.0 collective-permute-done.4.refs_1_
  17.4 1.6 %shard_map.86 = (f32[24,512]{1,0:T(8,128)S(1)}, bf16[256,512]{1,0:T(8,128)(2,1)S(1)}, bf16[256,512]{1,0:T(8,128)(2,1)S(1)}, bf16[512,128]{1,0:T(8,128)(2,1)S(1)}) custom-call(bf16[256,256]{1,0:T(8,128)(2,1)S(1)} %get-tuple-element.21.query_ref, bf16[256,256]{1,0:T(8,128)(2,1)S(1)} %get-tuple-element.22.grad_ref, ...), custom_call_target="tpu_custom_call" | custom-call | flops 536870912 | bytes 1540096 | tf_op jit(solution)/shard_map/pallas_call | solution.py:313
  19.0 1.5 %shard_map.87 = f32[24,512]{1,0:T(8,128)S(1)} custom-call(bf16[256,512]{1,0:T(8,128)(2,1)S(1)} %constant_dynamic-update-slice_fusion.2.chunk_ref, bf16[512,128]{1,0:T(8,128)(2,1)S(1)} %get-tuple-element.25.bias_ref, bf16[256,512]{1,0:T(8,128)(2,1)S(1)} %get-tuple-element.26.query_t_ref, bf16[256,512]{1,0:T(8,128)(2,1)S(1)} %get-tuple-element.27.grad_t_ref, ...), custom_call_target="tpu_custom_call" | custom-call | flops 536870912 | bytes 1015808 | tf_op jit(solution)/shard_map/pallas_call | solution.py:313
  20.5 0.1 collective-permute-start.6
  20.6 1.2 %collective-permute-done.6 = f32[24,512]{1,0:T(8,128)S(1)} collective-permute-done((f32[24,512]{1,0:T(8,128)S(1)}, f32[24,512]{1,0:T(8,128)S(1)}, u32[]{:S(2)}, u32[]{:S(2)}) %collective-permute-start.6) | collective-permute-done | bytes 49184 | tf_op jit(solution)/shard_map/ppermute | solution.py:359
  21.9 1.8 %collective-permute-start.7 = (f32[16,512]{1,0:T(8,128)S(1)}, f32[16,512]{1,0:T(8,128)S(1)}, u32[]{:S(2)}, u32[]{:S(2)}) collective-permute-start(f32[16,512]{1,0:T(8,128)S(1)} %pad_maximum_fusion.1.near_ref), channel_id=1, source_target_pairs={{0,8},{1,9},{2,10},{3,11},{4,12},{5,13},{6,14},{7,15},{8,0},{9,1},... | collective-permute-start | bytes 98312 | tf_op jit(solution)/shard_map/ppermute | solution.py:350
  23.7 1.2 %shard_map.88 = (f32[256,4096]{1,0:T(8,128)S(1)}, f32[256,4096]{1,0:T(8,128)S(1)}) custom-call(f32[16,512]{1,0:T(8,128)S(1)} %pad_maximum_fusion.1.near_ref, bf16[256,512]{1,0:T(8,128)(2,1)S(1)} %constant_dynamic-update-slice_fusion.2.chunk_ref, bf16[512,128]{1,0:T(8,128)(2,1)S(1)} %get-tuple-element.25.bias_ref, ...), custom_call_target="tpu_custom_call" | custom-call | flops 536870912 | bytes 9338880 | tf_op jit(solution)/shard_map/pallas_call | solution.py:313
  24.9 2.1 %collective-permute-done.7.across_ref = f32[16,512]{1,0:T(8,128)S(1)} collective-permute-done((f32[16,512]{1,0:T(8,128)S(1)}, f32[16,512]{1,0:T(8,128)S(1)}, u32[]{:S(2)}, u32[]{:S(2)}) %collective-permute-start.7) | collective-permute-done | bytes 32800 | tf_op jit(solution)/shard_map/ppermute | solution.py:350
  27.0 1.8 %shard_map.89 = (bf16[256,512]{1,0:T(8,128)(2,1)S(1)}, f32[256,512]{1,0:T(8,128)S(1)}, f32[16,512]{1,0:T(8,128)S(1)}) custom-call(f32[16,512]{1,0:T(8,128)S(1)} %pad_maximum_fusion.1.near_ref, f32[16,512]{1,0:T(8,128)S(1)} %collective-permute-done.7.across_ref, bf16[256,512]{1,0:T(8,128)(2,1)S(1)} %constant_dynamic-update-slice_fusion.2.chunk_ref, ...), custom_call_target="tpu_custom_call" | custom-call | flops 1342177280 | bytes 10059776 | tf_op jit(solution)/shard_map/pallas_call | solution.py:313
  28.8 2.5 %shard_map.90 = (f32[256,512]{1,0:T(8,128)S(1)}, f32[256,256]{1,0:T(8,128)S(1)}, bf16[256,256]{1,0:T(8,128)(2,1)S(1)}) custom-call(f32[16,512]{1,0:T(8,128)S(1)} %get-tuple-element.31.ends_ref, f32[256,512]{1,0:T(8,128)S(1)} %get-tuple-element.32.before_ref, bf16[256,512]{1,0:T(8,128)(2,1)S(1)} %constant_dynamic-update-slice_fusion.4.refs_2_.chunk_ref, ...), custom_call_target="tpu_custom_call" | custom-call | flops 1342177280 | bytes 2392064 | tf_op jit(solution)/shard_map/pallas_call | solution.py:313
  31.3 0.1 collective-permute-start.8
  31.4 1.3 %collective-permute-done.8 = bf16[256,256]{1,0:T(8,128)(2,1)S(1)} collective-permute-done((bf16[256,256]{1,0:T(8,128)(2,1)S(1)}, bf16[256,256]{1,0:T(8,128)(2,1)S(1)}, u32[]{:S(2)}, u32[]{:S(2)}) %collective-permute-start.8) | collective-permute-done | bytes 131104 | tf_op jit(solution)/shard_map/ppermute | solution.py:359
  32.8 1.6 %collective-permute-start.9 = (bf16[128,256]{1,0:T(8,128)(2,1)S(1)}, bf16[128,256]{1,0:T(8,128)(2,1)S(1)}, u32[]{:S(2)}, u32[]{:S(2)}) collective-permute-start(bf16[128,256]{1,0:T(8,128)(2,1)S(1)} %slice.133), channel_id=1, source_target_pairs={{0,8},{1,9},{2,10},{3,11},{4,12},{5,13},{6,14},{7,15},{8,0},{9,1},... | collective-permute-start | bytes 196616 | tf_op jit(solution)/shard_map/ppermute | solution.py:350
  34.4 4.9 %collective-permute-done.9 = bf16[128,256]{1,0:T(8,128)(2,1)S(1)} collective-permute-done((bf16[128,256]{1,0:T(8,128)(2,1)S(1)}, bf16[128,256]{1,0:T(8,128)(2,1)S(1)}, u32[]{:S(2)}, u32[]{:S(2)}) %collective-permute-start.9) | collective-permute-done | bytes 65568 | tf_op jit(solution)/shard_map/ppermute | solution.py:350
  39.3 0.1 collective-permute-start.10
  39.4 0.9 %collective-permute-start.11 = (bf16[256,512]{1,0:T(8,128)(2,1)S(1)}, bf16[256,512]{1,0:T(8,128)(2,1)S(1)}, u32[]{:S(2)}, u32[]{:S(2)}) collective-permute-start(bf16[256,512]{1,0:T(8,128)(2,1)S(1)} %get-tuple-element.36), channel_id=1, source_target_pairs={{0,2},{1,3},{2,0},{3,1},{4,6},{5,7},{6,4},{7,5},{8,10},{9,11},{10,... | collective-permute-start | bytes 786440 | tf_op jit(solution)/shard_map/ppermute | solution.py:350
  40.3 0.4 collective-permute-done.10
  40.7 5.2 %collective-permute-done.11 = bf16[256,512]{1,0:T(8,128)(2,1)S(1)} collective-permute-done((bf16[256,512]{1,0:T(8,128)(2,1)S(1)}, bf16[256,512]{1,0:T(8,128)(2,1)S(1)}, u32[]{:S(2)}, u32[]{:S(2)}) %collective-permute-start.11) | collective-permute-done | bytes 262176 | tf_op jit(solution)/shard_map/ppermute | solution.py:350
  45.8 0.1 fusion.7
  45.9 0.6 %collective-permute-start.12 = (bf16[64,512]{1,0:T(8,128)(2,1)S(1)}, bf16[64,512]{1,0:T(8,128)(2,1)S(1)}, u32[]{:S(2)}, u32[]{:S(2)}) collective-permute-start(bf16[64,512]{1,0:T(8,128)(2,1)S(1)} %get-tuple-element.39), channel_id=1, source_target_pairs={{0,5},{1,4},{2,7},{3,6},{4,1},{5,0},{6,3},{7,2},{8,13},{9,12},{10,... | collective-permute-start | bytes 196616 | tf_op jit(solution)/shard_map/ppermute | solution.py:350
  46.5 2.5 %collective-permute-start.13 = (bf16[64,512]{1,0:T(8,128)(2,1)S(1)}, bf16[64,512]{1,0:T(8,128)(2,1)S(1)}, u32[]{:S(2)}, u32[]{:S(2)}) collective-permute-start(bf16[64,512]{1,0:T(8,128)(2,1)S(1)} %get-tuple-element.41), channel_id=1, source_target_pairs={{0,4},{1,5},{2,6},{3,7},{4,0},{5,1},{6,2},{7,3},{8,12},{9,13},{10,... | collective-permute-start | bytes 196616 | tf_op jit(solution)/shard_map/ppermute | solution.py:350
  49.0 0.5 collective-permute-start.14
  49.5 0.7 %pad_maximum_fusion = bf16[256,256]{1,0:T(8,128)(2,1)} fusion(bf16[128,256]{1,0:T(8,128)(2,1)S(1)} %get-tuple-element.43, bf16[128,256]{1,0:T(8,128)(2,1)S(1)} %get-tuple-element.42), kind=kLoop, calls=%fused_computation.9 | loop fusion | flops 262144 | bytes 262144 | tf_op jit(solution)/shard_map/concatenate | solution.py:460
  50.2 1.6 %collective-permute-done.12 = bf16[64,512]{1,0:T(8,128)(2,1)S(1)} collective-permute-done((bf16[64,512]{1,0:T(8,128)(2,1)S(1)}, bf16[64,512]{1,0:T(8,128)(2,1)S(1)}, u32[]{:S(2)}, u32[]{:S(2)}) %collective-permute-start.12) | collective-permute-done | bytes 65568 | tf_op jit(solution)/shard_map/ppermute | solution.py:350
  51.7 0.2 collective-permute-done.13
  52.0 1.3 %collective-permute-done.14 = bf16[64,512]{1,0:T(8,128)(2,1)S(1)} collective-permute-done((bf16[64,512]{1,0:T(8,128)(2,1)S(1)}, bf16[64,512]{1,0:T(8,128)(2,1)S(1)}, u32[]{:S(2)}, u32[]{:S(2)}) %collective-permute-start.14) | collective-permute-done | bytes 65568 | tf_op jit(solution)/shard_map/ppermute | solution.py:350
  53.3 0.6 %fusion.9 = (bf16[64,256]{1,0:T(8,128)(2,1)}, bf16[64,256]{1,0:T(8,128)(2,1)}) fusion(bf16[64,512]{1,0:T(8,128)(2,1)S(1)} %fusion.2), kind=kLoop, calls=%fused_computation.33 | loop fusion | bytes 131072 | tf_op jit(solution)/shard_map/slice | solution.py:461
  (13 shorter events, 0.2 us)
Async XLA Ops:
  1.7 5.6 %collective-permute-start = (bf16[64,512]{1,0:T(8,128)(2,1)S(1)}, bf16[64,512]{1,0:T(8,128)(2,1)S(1)}, u32[]{:S(2)}, u32[]{:S(2)}) collective-permute-start(bf16[64,512]{1,0:T(8,128)(2,1)S(1)} %get-tuple-element.20), channel_id=1, source_target_pairs={{0,1},{1,0},{2,3},{3,2},{4,5},{5,4},{6,7},{7,6},{8,9},{9,8},{10,11... | collective-permute-start | bytes 196616 | tf_op jit(solution)/shard_map/ppermute | solution.py:350
  4.7 9.2 %collective-permute-start.3 = (bf16[272,256]{1,0:T(8,128)(2,1)S(1)}, bf16[272,256]{1,0:T(8,128)(2,1)S(1)}, u32[]{:S(2)}, u32[]{:S(2)}) collective-permute-start(bf16[272,256]{1,0:T(8,128)(2,1)S(1)} %get-tuple-element.23), channel_id=1, source_target_pairs={{0,8},{1,9},{2,10},{3,11},{4,12},{5,13},{6,14},{7,15},{8,0},{9,1},... | collective-permute-start | bytes 417800 | tf_op jit(solution)/shard_map/ppermute | solution.py:350
  7.3 7.4 %collective-permute-start.1 = (bf16[128,512]{1,0:T(8,128)(2,1)S(1)}, bf16[128,512]{1,0:T(8,128)(2,1)S(1)}, u32[]{:S(2)}, u32[]{:S(2)}) collective-permute-start(bf16[128,512]{1,0:T(8,128)(2,1)S(1)} %get-tuple-element.49), channel_id=1, source_target_pairs={{0,2},{1,3},{2,0},{3,1},{4,6},{5,7},{6,4},{7,5},{8,10},{9,11},{10,... | collective-permute-start | bytes 393224 | tf_op jit(solution)/shard_map/ppermute | solution.py:350
  9.1 6.1 %collective-permute-start.5 = (bf16[128,512]{1,0:T(8,128)(2,1)S(1)}, bf16[128,512]{1,0:T(8,128)(2,1)S(1)}, u32[]{:S(2)}, u32[]{:S(2)}) collective-permute-start(bf16[128,512]{1,0:T(8,128)(2,1)S(1)} %get-tuple-element.49), channel_id=1, source_target_pairs={{0,4},{1,5},{2,6},{3,7},{4,0},{5,1},{6,2},{7,3},{8,12},{9,13},{10,... | collective-permute-start | bytes 393224 | tf_op jit(solution)/shard_map/ppermute | solution.py:350
  10.7 6.7 %collective-permute-start.2 = (bf16[128,512]{1,0:T(8,128)(2,1)S(1)}, bf16[128,512]{1,0:T(8,128)(2,1)S(1)}, u32[]{:S(2)}, u32[]{:S(2)}) collective-permute-start(bf16[128,512]{1,0:T(8,128)(2,1)S(1)} %get-tuple-element.49), channel_id=1, source_target_pairs={{0,6},{1,7},{2,4},{3,5},{4,2},{5,3},{6,0},{7,1},{8,14},{9,15},{10,... | collective-permute-start | bytes 393224 | tf_op jit(solution)/shard_map/ppermute | solution.py:350
  13.9 3.5 %collective-permute-start.4 = (bf16[272,256]{1,0:T(8,128)(2,1)S(1)}, bf16[272,256]{1,0:T(8,128)(2,1)S(1)}, u32[]{:S(2)}, u32[]{:S(2)}) collective-permute-start(bf16[272,256]{1,0:T(8,128)(2,1)S(1)} %collective-permute-done.3.refs_0_), channel_id=1, source_target_pairs={{0,16},{16,0},{1,17},{17,1},{2,18},{18,2},{3,19},{19,3},{4,20},{20... | collective-permute-start | bytes 417800 | tf_op jit(solution)/shard_map/ppermute | solution.py:359
  20.5 1.3 %collective-permute-start.6 = (f32[24,512]{1,0:T(8,128)S(1)}, f32[24,512]{1,0:T(8,128)S(1)}, u32[]{:S(2)}, u32[]{:S(2)}) collective-permute-start(f32[24,512]{1,0:T(8,128)S(1)} %shard_map.87), channel_id=1, source_target_pairs={{0,16},{16,0},{1,17},{17,1},{2,18},{18,2},{3,19},{19,3},{4,20},{20... | collective-permute-start | bytes 147464 | tf_op jit(solution)/shard_map/ppermute | solution.py:359
  21.9 5.1 %collective-permute-start.7 = (f32[16,512]{1,0:T(8,128)S(1)}, f32[16,512]{1,0:T(8,128)S(1)}, u32[]{:S(2)}, u32[]{:S(2)}) collective-permute-start(f32[16,512]{1,0:T(8,128)S(1)} %pad_maximum_fusion.1.near_ref), channel_id=1, source_target_pairs={{0,8},{1,9},{2,10},{3,11},{4,12},{5,13},{6,14},{7,15},{8,0},{9,1},... | collective-permute-start | bytes 98312 | tf_op jit(solution)/shard_map/ppermute | solution.py:350
  31.3 1.4 %collective-permute-start.8 = (bf16[256,256]{1,0:T(8,128)(2,1)S(1)}, bf16[256,256]{1,0:T(8,128)(2,1)S(1)}, u32[]{:S(2)}, u32[]{:S(2)}) collective-permute-start(bf16[256,256]{1,0:T(8,128)(2,1)S(1)} %get-tuple-element.34), channel_id=1, source_target_pairs={{0,16},{16,0},{1,17},{17,1},{2,18},{18,2},{3,19},{19,3},{4,20},{20... | collective-permute-start | bytes 393224 | tf_op jit(solution)/shard_map/ppermute | solution.py:359
  32.8 6.5 %collective-permute-start.9 = (bf16[128,256]{1,0:T(8,128)(2,1)S(1)}, bf16[128,256]{1,0:T(8,128)(2,1)S(1)}, u32[]{:S(2)}, u32[]{:S(2)}) collective-permute-start(bf16[128,256]{1,0:T(8,128)(2,1)S(1)} %slice.133), channel_id=1, source_target_pairs={{0,8},{1,9},{2,10},{3,11},{4,12},{5,13},{6,14},{7,15},{8,0},{9,1},... | collective-permute-start | bytes 196616 | tf_op jit(solution)/shard_map/ppermute | solution.py:350
  39.3 1.3 %collective-permute-start.10 = (bf16[128,256]{1,0:T(8,128)(2,1)S(1)}, bf16[128,256]{1,0:T(8,128)(2,1)S(1)}, u32[]{:S(2)}, u32[]{:S(2)}) collective-permute-start(bf16[128,256]{1,0:T(8,128)(2,1)S(1)} %fusion.3), channel_id=1, source_target_pairs={{0,16},{16,0},{1,17},{17,1},{2,18},{18,2},{3,19},{19,3},{4,20},{20... | collective-permute-start | bytes 196616 | tf_op jit(solution)/shard_map/ppermute | solution.py:359
  39.4 6.4 %collective-permute-start.11 = (bf16[256,512]{1,0:T(8,128)(2,1)S(1)}, bf16[256,512]{1,0:T(8,128)(2,1)S(1)}, u32[]{:S(2)}, u32[]{:S(2)}) collective-permute-start(bf16[256,512]{1,0:T(8,128)(2,1)S(1)} %get-tuple-element.36), channel_id=1, source_target_pairs={{0,2},{1,3},{2,0},{3,1},{4,6},{5,7},{6,4},{7,5},{8,10},{9,11},{10,... | collective-permute-start | bytes 786440 | tf_op jit(solution)/shard_map/ppermute | solution.py:350
  45.9 5.8 %collective-permute-start.12 = (bf16[64,512]{1,0:T(8,128)(2,1)S(1)}, bf16[64,512]{1,0:T(8,128)(2,1)S(1)}, u32[]{:S(2)}, u32[]{:S(2)}) collective-permute-start(bf16[64,512]{1,0:T(8,128)(2,1)S(1)} %get-tuple-element.39), channel_id=1, source_target_pairs={{0,5},{1,4},{2,7},{3,6},{4,1},{5,0},{6,3},{7,2},{8,13},{9,12},{10,... | collective-permute-start | bytes 196616 | tf_op jit(solution)/shard_map/ppermute | solution.py:350
  46.5 5.4 %collective-permute-start.13 = (bf16[64,512]{1,0:T(8,128)(2,1)S(1)}, bf16[64,512]{1,0:T(8,128)(2,1)S(1)}, u32[]{:S(2)}, u32[]{:S(2)}) collective-permute-start(bf16[64,512]{1,0:T(8,128)(2,1)S(1)} %get-tuple-element.41), channel_id=1, source_target_pairs={{0,4},{1,5},{2,6},{3,7},{4,0},{5,1},{6,2},{7,3},{8,12},{9,13},{10,... | collective-permute-start | bytes 196616 | tf_op jit(solution)/shard_map/ppermute | solution.py:350
  49.0 4.3 %collective-permute-start.14 = (bf16[64,512]{1,0:T(8,128)(2,1)S(1)}, bf16[64,512]{1,0:T(8,128)(2,1)S(1)}, u32[]{:S(2)}, u32[]{:S(2)}) collective-permute-start(bf16[64,512]{1,0:T(8,128)(2,1)S(1)} %get-tuple-element.40), channel_id=1, source_target_pairs={{0,1},{1,0},{2,3},{3,2},{4,5},{5,4},{6,7},{7,6},{8,9},{9,8},{10,11... | collective-permute-start | bytes 196616 | tf_op jit(solution)/shard_map/ppermute | solution.py:350

commit v3 on v2

--- a/solution.py
+++ b/solution.py
@@ -188,9 +188,12 @@
     return [(head, slice(first, first + span)) for head in range(H) for first in range(0, queries, span)]
 
 
-def near_kernel(span, tile_rows, factor, near_ref, chunk_ref, bias_ref, query_t_ref, grad_t_ref, weights_ref, dprobs_ref):
+def near_kernel(span, tile_rows, factor, near_ref, chunk_ref, held_ref, bias_ref, query_t_ref, grad_t_ref, weights_ref,
+                dprobs_ref, keys_t_ref, held_t_ref):
     width, queries = query_t_ref.shape
     keys, values = chunk_of(chunk_ref, width)
+    keys_t_ref[...] = chunk_ref[:, :width].T
+    held_t_ref[...] = held_ref[:, :width].T
     bias = bias_ref[chunk_ref.shape[0] :, :]
     blocks = block_list(queries, span)
 
@@ -242,9 +245,9 @@
     return products
 
 
-def third_kernel(span, scale, near_ref, across_ref, chunk_ref, query_t_ref, grad_t_ref, weights_ref, dprobs_ref,
+def third_kernel(span, scale, near_ref, across_ref, keys_t_ref, query_t_ref, grad_t_ref, weights_ref, dprobs_ref,
                  out_ref, query_sum_ref, ends_ref, shrink_ref):
-    width, queries = query_t_ref.shape
+    _, queries = query_t_ref.shape
     rows = queries // 2
     turned = jnp.concatenate((across_ref[:, rows:], across_ref[:, :rows]), axis=1)
     top = jnp.maximum(near_ref[:H, :], turned[:H, :])
@@ -254,7 +257,7 @@
     ends_ref[:H, :] = lse
     ends_ref[H:, :] = (near * near_ref[H:, :] + across * turned[H:, :]) / total
     shrink_ref[...] = jnp.exp2(near_ref[:H, :] - lse)
-    keys_t = chunk_ref[:, :width].T
+    keys_t = keys_t_ref[...]
     blocks = block_list(queries, span)
 
     def rounded(n):
@@ -268,12 +271,12 @@
     staggered(len(blocks), (rounded, products), (0, 1))
 
 
-def fourth_kernel(cams, span, tile_rows, factor, scale, ends_ref, before_ref, chunk_ref, bias_ref, query_t_ref,
+def fourth_kernel(cams, span, tile_rows, factor, scale, ends_ref, before_ref, chunk_ref, keys_t_ref, bias_ref, query_t_ref,
                   grad_t_ref, out_ref, keep_ref, *refs):
     turn_refs, (query_sum_ref, whole_ref) = refs[: cams - 1], refs[cams - 1 :]
     width, queries = query_t_ref.shape
     keys, values = chunk_of(chunk_ref, width)
-    keys_t = chunk_ref[:, :width].T
+    keys_t = keys_t_ref[...]
     bias = bias_ref[: chunk_ref.shape[0], :]
     blocks = block_list(queries, span)
 
@@ -413,17 +416,22 @@
     )
     near = combine([stats] + [turn(stats, shift) for shift in range(1, cams)], factor)
     opposite = swap_half(near)
-    weights, dprobs = run(
+    weights, dprobs, keys_t, held_t = run(
         functools.partial(near_kernel, span, tile_rows, factor),
-        (shape((chunk, H * all_rows), F32), shape((chunk, H * all_rows), F32)),
-        (near, last, bias, query_t, grad_t),
+        (
+            shape((chunk, H * all_rows), F32),
+            shape((chunk, H * all_rows), F32),
+            shape((width, chunk), BF16),
+            shape((width, chunk), BF16),
+        ),
+        (near, last, held, bias, query_t, grad_t),
         flops=8 * work,
     )
 
     sent, query_sum, ends = run(
         functools.partial(third_kernel, span, scale),
         (shape((chunk, 2 * width), BF16), shape((width, all_rows), F32), shape((2 * H, all_rows), F32)),
-        (near, opposite, last, query_t, grad_t, weights, dprobs),
+        (near, opposite, keys_t, query_t, grad_t, weights, dprobs),
         scratch=(pltpu.VMEM((H, all_rows), F32),),
         flops=20 * work,
     )
@@ -436,7 +444,7 @@
             shape((2 * part, width), F32),
             *(shape((2 * part, width), BF16) for _ in range(1, cams)),
         ),
-        (ends, query_sum, held, bias, query_t, grad_t),
+        (ends, query_sum, held, held_t, bias, query_t, grad_t),
         scratch=(pltpu.VMEM((width, all_rows), F32), pltpu.VMEM((all_rows, width), F32)),
             flops=20 * work,
     )

time: 54.1 us -> 54.1 us (level)
  no operation moved by 1% of the time
where the time goes in v3:
time: 54.1 us; the launch traced here: 54 us
  waiting for transfers between devices  24.7 us (46%)
  starting transfers between devices  17.2 us (32%)
  Pallas kernels  9.78 us (18%)
  other arithmetic  0.86 us (2%)
  between operations  0.8 us (1%)
  local copies, waits for them, and re-layouts  0.7 us (1%)
    ppermute x11, waiting for transfers between devices, across(): return lax.ppermute(x, ('cam', 'tile'), pairs)  21.7 us
    ppermute x11, starting transfers between devices, across(): return lax.ppermute(x, ('cam', 'tile'), pairs)  17 us
    pallas_call x6, Pallas kernels, run(): pl.pallas_call(kernel, out_shape=tuple(outs), in_specs=[pl.BlockSpec(memo...  9.78 us
    ppermute x4, waiting for transfers between devices, turn(): lax.ppermute(x, 'cam', [(c, (c + shift) % cams) for c in range(cams)])  2.91 us
  transfers between devices with their start and end apart: 15, of which 13 were waited for; matrix products, arithmetic and copies ran while one was open for 1% of the time, Pallas kernels for 2%

profile of v3, /device:TPU:0, one launch (start us, length us, event | category | flops | bytes accessed | tf_op | source)
XLA Modules:
  0.0 54.0 jit_solution(5608289119757473705)
XLA Ops:
  0.6 1.0 %shard_map.85 = (bf16[64,512]{1,0:T(8,128)(2,1)S(1)}, bf16[256,256]{1,0:T(8,128)(2,1)S(1)}, bf16[256,256]{1,0:T(8,128)(2,1)S(1)}, bf16[272,256]{1,0:T(8,128)(2,1)S(1)}, bf16[128,128]{1,0:T(8,128)(2,1)S(1)}) custom-call(bf16[64,256]{1,0:T(8,128)(2,1)} %key_ref.1, bf16[64,256]{1,0:T(8,128)(2,1)} %value_ref.1, bf16[256,256]{1,0:T(8,128)(2,1)} %query_ref.1, ...), custom_call_target="tpu_custom_call" | custom-call | bytes 827776 | tf_op jit(solution)/shard_map/pallas_call | solution.py:316
  1.7 3.0 %collective-permute-start = (bf16[64,512]{1,0:T(8,128)(2,1)S(1)}, bf16[64,512]{1,0:T(8,128)(2,1)S(1)}, u32[]{:S(2)}, u32[]{:S(2)}) collective-permute-start(bf16[64,512]{1,0:T(8,128)(2,1)S(1)} %get-tuple-element.22), channel_id=1, source_target_pairs={{0,1},{1,0},{2,3},{3,2},{4,5},{5,4},{6,7},{7,6},{8,9},{9,8},{10,11... | collective-permute-start | bytes 196616 | tf_op jit(solution)/shard_map/ppermute | solution.py:353
  4.7 2.6 %collective-permute-start.3 = (bf16[272,256]{1,0:T(8,128)(2,1)S(1)}, bf16[272,256]{1,0:T(8,128)(2,1)S(1)}, u32[]{:S(2)}, u32[]{:S(2)}) collective-permute-start(bf16[272,256]{1,0:T(8,128)(2,1)S(1)} %get-tuple-element.25), channel_id=1, source_target_pairs={{0,8},{1,9},{2,10},{3,11},{4,12},{5,13},{6,14},{7,15},{8,0},{9,1},... | collective-permute-start | bytes 417800 | tf_op jit(solution)/shard_map/ppermute | solution.py:353
  7.3 0.0 collective-permute-done
  7.3 1.7 %collective-permute-start.1 = (bf16[128,512]{1,0:T(8,128)(2,1)S(1)}, bf16[128,512]{1,0:T(8,128)(2,1)S(1)}, u32[]{:S(2)}, u32[]{:S(2)}) collective-permute-start(bf16[128,512]{1,0:T(8,128)(2,1)S(1)} %get-tuple-element.53), channel_id=1, source_target_pairs={{0,2},{1,3},{2,0},{3,1},{4,6},{5,7},{6,4},{7,5},{8,10},{9,11},{10,... | collective-permute-start | bytes 393224 | tf_op jit(solution)/shard_map/ppermute | solution.py:353
  9.1 1.6 %collective-permute-start.5 = (bf16[128,512]{1,0:T(8,128)(2,1)S(1)}, bf16[128,512]{1,0:T(8,128)(2,1)S(1)}, u32[]{:S(2)}, u32[]{:S(2)}) collective-permute-start(bf16[128,512]{1,0:T(8,128)(2,1)S(1)} %get-tuple-element.53), channel_id=1, source_target_pairs={{0,4},{1,5},{2,6},{3,7},{4,0},{5,1},{6,2},{7,3},{8,12},{9,13},{10,... | collective-permute-start | bytes 393224 | tf_op jit(solution)/shard_map/ppermute | solution.py:353
  10.7 0.2 collective-permute-start.2
  10.9 3.0 %collective-permute-done.3.refs_0_ = bf16[272,256]{1,0:T(8,128)(2,1)S(1)} collective-permute-done((bf16[272,256]{1,0:T(8,128)(2,1)S(1)}, bf16[272,256]{1,0:T(8,128)(2,1)S(1)}, u32[]{:S(2)}, u32[]{:S(2)}) %collective-permute-start.3) | collective-permute-done | bytes 139296 | tf_op jit(solution)/shard_map/ppermute | solution.py:353
  13.9 0.0 collective-permute-start.4
  13.9 0.9 %collective-permute-done.1 = bf16[128,512]{1,0:T(8,128)(2,1)S(1)} collective-permute-done((bf16[128,512]{1,0:T(8,128)(2,1)S(1)}, bf16[128,512]{1,0:T(8,128)(2,1)S(1)}, u32[]{:S(2)}, u32[]{:S(2)}) %collective-permute-start.1) | collective-permute-done | bytes 131104 | tf_op jit(solution)/shard_map/ppermute | solution.py:353
  14.8 0.4 collective-permute-done.5
  15.2 2.1 %collective-permute-done.2 = bf16[128,512]{1,0:T(8,128)(2,1)S(1)} collective-permute-done((bf16[128,512]{1,0:T(8,128)(2,1)S(1)}, bf16[128,512]{1,0:T(8,128)(2,1)S(1)}, u32[]{:S(2)}, u32[]{:S(2)}) %collective-permute-start.2) | collective-permute-done | bytes 131104 | tf_op jit(solution)/shard_map/ppermute | solution.py:353
  17.4 0.0 collective-permute-done.4.refs_1_
  17.4 1.6 %shard_map.86 = (f32[24,512]{1,0:T(8,128)S(1)}, bf16[256,512]{1,0:T(8,128)(2,1)S(1)}, bf16[256,512]{1,0:T(8,128)(2,1)S(1)}, bf16[512,128]{1,0:T(8,128)(2,1)S(1)}) custom-call(bf16[256,256]{1,0:T(8,128)(2,1)S(1)} %get-tuple-element.23.query_ref, bf16[256,256]{1,0:T(8,128)(2,1)S(1)} %get-tuple-element.24.grad_ref, ...), custom_call_target="tpu_custom_call" | custom-call | flops 536870912 | bytes 1540096 | tf_op jit(solution)/shard_map/pallas_call | solution.py:316
  19.0 1.6 %shard_map.87 = f32[24,512]{1,0:T(8,128)S(1)} custom-call(bf16[256,512]{1,0:T(8,128)(2,1)S(1)} %constant_dynamic-update-slice_fusion.2.chunk_ref, bf16[512,128]{1,0:T(8,128)(2,1)S(1)} %get-tuple-element.27.bias_ref, bf16[256,512]{1,0:T(8,128)(2,1)S(1)} %get-tuple-element.28.query_t_ref, bf16[256,512]{1,0:T(8,128)(2,1)S(1)} %get-tuple-element.29.grad_t_ref, ...), custom_call_target="tpu_custom_call" | custom-call | flops 536870912 | bytes 1015808 | tf_op jit(solution)/shard_map/pallas_call | solution.py:316
  20.6 0.1 collective-permute-start.6
  20.7 1.2 %collective-permute-done.6 = f32[24,512]{1,0:T(8,128)S(1)} collective-permute-done((f32[24,512]{1,0:T(8,128)S(1)}, f32[24,512]{1,0:T(8,128)S(1)}, u32[]{:S(2)}, u32[]{:S(2)}) %collective-permute-start.6) | collective-permute-done | bytes 49184 | tf_op jit(solution)/shard_map/ppermute | solution.py:362
  21.9 1.8 %collective-permute-start.7 = (f32[16,512]{1,0:T(8,128)S(1)}, f32[16,512]{1,0:T(8,128)S(1)}, u32[]{:S(2)}, u32[]{:S(2)}) collective-permute-start(f32[16,512]{1,0:T(8,128)S(1)} %pad_maximum_fusion.1.near_ref), channel_id=1, source_target_pairs={{0,8},{1,9},{2,10},{3,11},{4,12},{5,13},{6,14},{7,15},{8,0},{9,1},... | collective-permute-start | bytes 98312 | tf_op jit(solution)/shard_map/ppermute | solution.py:353
  23.8 1.2 %shard_map.88 = (f32[256,4096]{1,0:T(8,128)S(1)}, f32[256,4096]{1,0:T(8,128)S(1)}, bf16[256,256]{1,0:T(8,128)(2,1)S(1)}, bf16[256,256]{1,0:T(8,128)(2,1)S(1)}) custom-call(f32[16,512]{1,0:T(8,128)S(1)} %pad_maximum_fusion.1.near_ref, bf16[256,512]{1,0:T(8,128)(2,1)S(1)} %constant_dynamic-update-slice_fusion.2.chunk_ref, ...), custom_call_target="tpu_custom_call" | custom-call | flops 536870912 | bytes 9863168 | tf_op jit(solution)/shard_map/pallas_call | solution.py:316
  25.0 2.1 %collective-permute-done.7.across_ref = f32[16,512]{1,0:T(8,128)S(1)} collective-permute-done((f32[16,512]{1,0:T(8,128)S(1)}, f32[16,512]{1,0:T(8,128)S(1)}, u32[]{:S(2)}, u32[]{:S(2)}) %collective-permute-start.7) | collective-permute-done | bytes 32800 | tf_op jit(solution)/shard_map/ppermute | solution.py:353
  27.1 1.8 %shard_map.89 = (bf16[256,512]{1,0:T(8,128)(2,1)S(1)}, f32[256,512]{1,0:T(8,128)S(1)}, f32[16,512]{1,0:T(8,128)S(1)}) custom-call(f32[16,512]{1,0:T(8,128)S(1)} %pad_maximum_fusion.1.near_ref, f32[16,512]{1,0:T(8,128)S(1)} %collective-permute-done.7.across_ref, bf16[256,256]{1,0:T(8,128)(2,1)S(1)} %get-tuple-element.31.keys_t_ref, ...), custom_call_target="tpu_custom_call" | custom-call | flops 1342177280 | bytes 9928704 | tf_op jit(solution)/shard_map/pallas_call | solution.py:316
  28.9 2.5 %shard_map.90 = (f32[256,512]{1,0:T(8,128)S(1)}, f32[256,256]{1,0:T(8,128)S(1)}, bf16[256,256]{1,0:T(8,128)(2,1)S(1)}) custom-call(f32[16,512]{1,0:T(8,128)S(1)} %get-tuple-element.34.ends_ref, f32[256,512]{1,0:T(8,128)S(1)} %get-tuple-element.35.before_ref, bf16[256,512]{1,0:T(8,128)(2,1)S(1)} %constant_dynamic-update-slice_fusion.4.refs_2_.held_ref.chunk_ref, ...), custom_call_target="tpu_custom_call" | custom-call | flops 1342177280 | bytes 2523136 | tf_op jit(solution)/shard_map/pallas_call | solution.py:316
  31.4 0.1 collective-permute-start.8
  31.5 1.3 %collective-permute-done.8 = bf16[256,256]{1,0:T(8,128)(2,1)S(1)} collective-permute-done((bf16[256,256]{1,0:T(8,128)(2,1)S(1)}, bf16[256,256]{1,0:T(8,128)(2,1)S(1)}, u32[]{:S(2)}, u32[]{:S(2)}) %collective-permute-start.8) | collective-permute-done | bytes 131104 | tf_op jit(solution)/shard_map/ppermute | solution.py:362
  32.8 1.6 %collective-permute-start.9 = (bf16[128,256]{1,0:T(8,128)(2,1)S(1)}, bf16[128,256]{1,0:T(8,128)(2,1)S(1)}, u32[]{:S(2)}, u32[]{:S(2)}) collective-permute-start(bf16[128,256]{1,0:T(8,128)(2,1)S(1)} %slice.133), channel_id=1, source_target_pairs={{0,8},{1,9},{2,10},{3,11},{4,12},{5,13},{6,14},{7,15},{8,0},{9,1},... | collective-permute-start | bytes 196616 | tf_op jit(solution)/shard_map/ppermute | solution.py:353
  34.4 4.9 %collective-permute-done.9 = bf16[128,256]{1,0:T(8,128)(2,1)S(1)} collective-permute-done((bf16[128,256]{1,0:T(8,128)(2,1)S(1)}, bf16[128,256]{1,0:T(8,128)(2,1)S(1)}, u32[]{:S(2)}, u32[]{:S(2)}) %collective-permute-start.9) | collective-permute-done | bytes 65568 | tf_op jit(solution)/shard_map/ppermute | solution.py:353
  39.4 0.1 collective-permute-start.10
  39.5 0.9 %collective-permute-start.11 = (bf16[256,512]{1,0:T(8,128)(2,1)S(1)}, bf16[256,512]{1,0:T(8,128)(2,1)S(1)}, u32[]{:S(2)}, u32[]{:S(2)}) collective-permute-start(bf16[256,512]{1,0:T(8,128)(2,1)S(1)} %get-tuple-element.40), channel_id=1, source_target_pairs={{0,2},{1,3},{2,0},{3,1},{4,6},{5,7},{6,4},{7,5},{8,10},{9,11},{10,... | collective-permute-start | bytes 786440 | tf_op jit(solution)/shard_map/ppermute | solution.py:353
  40.3 0.4 collective-permute-done.10
  40.7 5.2 %collective-permute-done.11 = bf16[256,512]{1,0:T(8,128)(2,1)S(1)} collective-permute-done((bf16[256,512]{1,0:T(8,128)(2,1)S(1)}, bf16[256,512]{1,0:T(8,128)(2,1)S(1)}, u32[]{:S(2)}, u32[]{:S(2)}) %collective-permute-start.11) | collective-permute-done | bytes 262176 | tf_op jit(solution)/shard_map/ppermute | solution.py:353
  45.9 0.1 fusion.7
  46.0 0.6 %collective-permute-start.12 = (bf16[64,512]{1,0:T(8,128)(2,1)S(1)}, bf16[64,512]{1,0:T(8,128)(2,1)S(1)}, u32[]{:S(2)}, u32[]{:S(2)}) collective-permute-start(bf16[64,512]{1,0:T(8,128)(2,1)S(1)} %get-tuple-element.43), channel_id=1, source_target_pairs={{0,5},{1,4},{2,7},{3,6},{4,1},{5,0},{6,3},{7,2},{8,13},{9,12},{10,... | collective-permute-start | bytes 196616 | tf_op jit(solution)/shard_map/ppermute | solution.py:353
  46.6 2.5 %collective-permute-start.13 = (bf16[64,512]{1,0:T(8,128)(2,1)S(1)}, bf16[64,512]{1,0:T(8,128)(2,1)S(1)}, u32[]{:S(2)}, u32[]{:S(2)}) collective-permute-start(bf16[64,512]{1,0:T(8,128)(2,1)S(1)} %get-tuple-element.45), channel_id=1, source_target_pairs={{0,4},{1,5},{2,6},{3,7},{4,0},{5,1},{6,2},{7,3},{8,12},{9,13},{10,... | collective-permute-start | bytes 196616 | tf_op jit(solution)/shard_map/ppermute | solution.py:353
  49.1 0.5 collective-permute-start.14
  49.6 0.7 %pad_maximum_fusion = bf16[256,256]{1,0:T(8,128)(2,1)} fusion(bf16[128,256]{1,0:T(8,128)(2,1)S(1)} %get-tuple-element.47, bf16[128,256]{1,0:T(8,128)(2,1)S(1)} %get-tuple-element.46), kind=kLoop, calls=%fused_computation.9 | loop fusion | flops 262144 | bytes 262144 | tf_op jit(solution)/shard_map/concatenate | solution.py:468
  50.2 1.6 %collective-permute-done.12 = bf16[64,512]{1,0:T(8,128)(2,1)S(1)} collective-permute-done((bf16[64,512]{1,0:T(8,128)(2,1)S(1)}, bf16[64,512]{1,0:T(8,128)(2,1)S(1)}, u32[]{:S(2)}, u32[]{:S(2)}) %collective-permute-start.12) | collective-permute-done | bytes 65568 | tf_op jit(solution)/shard_map/ppermute | solution.py:353
  51.8 0.2 collective-permute-done.13
  52.0 1.3 %collective-permute-done.14 = bf16[64,512]{1,0:T(8,128)(2,1)S(1)} collective-permute-done((bf16[64,512]{1,0:T(8,128)(2,1)S(1)}, bf16[64,512]{1,0:T(8,128)(2,1)S(1)}, u32[]{:S(2)}, u32[]{:S(2)}) %collective-permute-start.14) | collective-permute-done | bytes 65568 | tf_op jit(solution)/shard_map/ppermute | solution.py:353
  53.4 0.6 %fusion.9 = (bf16[64,256]{1,0:T(8,128)(2,1)}, bf16[64,256]{1,0:T(8,128)(2,1)}) fusion(bf16[64,512]{1,0:T(8,128)(2,1)S(1)} %fusion.2), kind=kLoop, calls=%fused_computation.33 | loop fusion | bytes 131072 | tf_op jit(solution)/shard_map/slice | solution.py:469
  (13 shorter events, 0.2 us)
Async XLA Ops:
  1.7 5.6 %collective-permute-start = (bf16[64,512]{1,0:T(8,128)(2,1)S(1)}, bf16[64,512]{1,0:T(8,128)(2,1)S(1)}, u32[]{:S(2)}, u32[]{:S(2)}) collective-permute-start(bf16[64,512]{1,0:T(8,128)(2,1)S(1)} %get-tuple-element.22), channel_id=1, source_target_pairs={{0,1},{1,0},{2,3},{3,2},{4,5},{5,4},{6,7},{7,6},{8,9},{9,8},{10,11... | collective-permute-start | bytes 196616 | tf_op jit(solution)/shard_map/ppermute | solution.py:353
  4.7 9.2 %collective-permute-start.3 = (bf16[272,256]{1,0:T(8,128)(2,1)S(1)}, bf16[272,256]{1,0:T(8,128)(2,1)S(1)}, u32[]{:S(2)}, u32[]{:S(2)}) collective-permute-start(bf16[272,256]{1,0:T(8,128)(2,1)S(1)} %get-tuple-element.25), channel_id=1, source_target_pairs={{0,8},{1,9},{2,10},{3,11},{4,12},{5,13},{6,14},{7,15},{8,0},{9,1},... | collective-permute-start | bytes 417800 | tf_op jit(solution)/shard_map/ppermute | solution.py:353
  7.3 7.4 %collective-permute-start.1 = (bf16[128,512]{1,0:T(8,128)(2,1)S(1)}, bf16[128,512]{1,0:T(8,128)(2,1)S(1)}, u32[]{:S(2)}, u32[]{:S(2)}) collective-permute-start(bf16[128,512]{1,0:T(8,128)(2,1)S(1)} %get-tuple-element.53), channel_id=1, source_target_pairs={{0,2},{1,3},{2,0},{3,1},{4,6},{5,7},{6,4},{7,5},{8,10},{9,11},{10,... | collective-permute-start | bytes 393224 | tf_op jit(solution)/shard_map/ppermute | solution.py:353
  9.1 6.1 %collective-permute-start.5 = (bf16[128,512]{1,0:T(8,128)(2,1)S(1)}, bf16[128,512]{1,0:T(8,128)(2,1)S(1)}, u32[]{:S(2)}, u32[]{:S(2)}) collective-permute-start(bf16[128,512]{1,0:T(8,128)(2,1)S(1)} %get-tuple-element.53), channel_id=1, source_target_pairs={{0,4},{1,5},{2,6},{3,7},{4,0},{5,1},{6,2},{7,3},{8,12},{9,13},{10,... | collective-permute-start | bytes 393224 | tf_op jit(solution)/shard_map/ppermute | solution.py:353
  10.7 6.7 %collective-permute-start.2 = (bf16[128,512]{1,0:T(8,128)(2,1)S(1)}, bf16[128,512]{1,0:T(8,128)(2,1)S(1)}, u32[]{:S(2)}, u32[]{:S(2)}) collective-permute-start(bf16[128,512]{1,0:T(8,128)(2,1)S(1)} %get-tuple-element.53), channel_id=1, source_target_pairs={{0,6},{1,7},{2,4},{3,5},{4,2},{5,3},{6,0},{7,1},{8,14},{9,15},{10,... | collective-permute-start | bytes 393224 | tf_op jit(solution)/shard_map/ppermute | solution.py:353
  13.9 3.5 %collective-permute-start.4 = (bf16[272,256]{1,0:T(8,128)(2,1)S(1)}, bf16[272,256]{1,0:T(8,128)(2,1)S(1)}, u32[]{:S(2)}, u32[]{:S(2)}) collective-permute-start(bf16[272,256]{1,0:T(8,128)(2,1)S(1)} %collective-permute-done.3.refs_0_), channel_id=1, source_target_pairs={{0,16},{16,0},{1,17},{17,1},{2,18},{18,2},{3,19},{19,3},{4,20},{20... | collective-permute-start | bytes 417800 | tf_op jit(solution)/shard_map/ppermute | solution.py:362
  20.6 1.3 %collective-permute-start.6 = (f32[24,512]{1,0:T(8,128)S(1)}, f32[24,512]{1,0:T(8,128)S(1)}, u32[]{:S(2)}, u32[]{:S(2)}) collective-permute-start(f32[24,512]{1,0:T(8,128)S(1)} %shard_map.87), channel_id=1, source_target_pairs={{0,16},{16,0},{1,17},{17,1},{2,18},{18,2},{3,19},{19,3},{4,20},{20... | collective-permute-start | bytes 147464 | tf_op jit(solution)/shard_map/ppermute | solution.py:362
  21.9 5.1 %collective-permute-start.7 = (f32[16,512]{1,0:T(8,128)S(1)}, f32[16,512]{1,0:T(8,128)S(1)}, u32[]{:S(2)}, u32[]{:S(2)}) collective-permute-start(f32[16,512]{1,0:T(8,128)S(1)} %pad_maximum_fusion.1.near_ref), channel_id=1, source_target_pairs={{0,8},{1,9},{2,10},{3,11},{4,12},{5,13},{6,14},{7,15},{8,0},{9,1},... | collective-permute-start | bytes 98312 | tf_op jit(solution)/shard_map/ppermute | solution.py:353
  31.4 1.4 %collective-permute-start.8 = (bf16[256,256]{1,0:T(8,128)(2,1)S(1)}, bf16[256,256]{1,0:T(8,128)(2,1)S(1)}, u32[]{:S(2)}, u32[]{:S(2)}) collective-permute-start(bf16[256,256]{1,0:T(8,128)(2,1)S(1)} %get-tuple-element.38), channel_id=1, source_target_pairs={{0,16},{16,0},{1,17},{17,1},{2,18},{18,2},{3,19},{19,3},{4,20},{20... | collective-permute-start | bytes 393224 | tf_op jit(solution)/shard_map/ppermute | solution.py:362
  32.8 6.5 %collective-permute-start.9 = (bf16[128,256]{1,0:T(8,128)(2,1)S(1)}, bf16[128,256]{1,0:T(8,128)(2,1)S(1)}, u32[]{:S(2)}, u32[]{:S(2)}) collective-permute-start(bf16[128,256]{1,0:T(8,128)(2,1)S(1)} %slice.133), channel_id=1, source_target_pairs={{0,8},{1,9},{2,10},{3,11},{4,12},{5,13},{6,14},{7,15},{8,0},{9,1},... | collective-permute-start | bytes 196616 | tf_op jit(solution)/shard_map/ppermute | solution.py:353
  39.4 1.3 %collective-permute-start.10 = (bf16[128,256]{1,0:T(8,128)(2,1)S(1)}, bf16[128,256]{1,0:T(8,128)(2,1)S(1)}, u32[]{:S(2)}, u32[]{:S(2)}) collective-permute-start(bf16[128,256]{1,0:T(8,128)(2,1)S(1)} %fusion.3), channel_id=1, source_target_pairs={{0,16},{16,0},{1,17},{17,1},{2,18},{18,2},{3,19},{19,3},{4,20},{20... | collective-permute-start | bytes 196616 | tf_op jit(solution)/shard_map/ppermute | solution.py:362
  39.5 6.4 %collective-permute-start.11 = (bf16[256,512]{1,0:T(8,128)(2,1)S(1)}, bf16[256,512]{1,0:T(8,128)(2,1)S(1)}, u32[]{:S(2)}, u32[]{:S(2)}) collective-permute-start(bf16[256,512]{1,0:T(8,128)(2,1)S(1)} %get-tuple-element.40), channel_id=1, source_target_pairs={{0,2},{1,3},{2,0},{3,1},{4,6},{5,7},{6,4},{7,5},{8,10},{9,11},{10,... | collective-permute-start | bytes 786440 | tf_op jit(solution)/shard_map/ppermute | solution.py:353
  46.0 5.8 %collective-permute-start.12 = (bf16[64,512]{1,0:T(8,128)(2,1)S(1)}, bf16[64,512]{1,0:T(8,128)(2,1)S(1)}, u32[]{:S(2)}, u32[]{:S(2)}) collective-permute-start(bf16[64,512]{1,0:T(8,128)(2,1)S(1)} %get-tuple-element.43), channel_id=1, source_target_pairs={{0,5},{1,4},{2,7},{3,6},{4,1},{5,0},{6,3},{7,2},{8,13},{9,12},{10,... | collective-permute-start | bytes 196616 | tf_op jit(solution)/shard_map/ppermute | solution.py:353
  46.6 5.4 %collective-permute-start.13 = (bf16[64,512]{1,0:T(8,128)(2,1)S(1)}, bf16[64,512]{1,0:T(8,128)(2,1)S(1)}, u32[]{:S(2)}, u32[]{:S(2)}) collective-permute-start(bf16[64,512]{1,0:T(8,128)(2,1)S(1)} %get-tuple-element.45), channel_id=1, source_target_pairs={{0,4},{1,5},{2,6},{3,7},{4,0},{5,1},{6,2},{7,3},{8,12},{9,13},{10,... | collective-permute-start | bytes 196616 | tf_op jit(solution)/shard_map/ppermute | solution.py:353
  49.1 4.3 %collective-permute-start.14 = (bf16[64,512]{1,0:T(8,128)(2,1)S(1)}, bf16[64,512]{1,0:T(8,128)(2,1)S(1)}, u32[]{:S(2)}, u32[]{:S(2)}) collective-permute-start(bf16[64,512]{1,0:T(8,128)(2,1)S(1)} %get-tuple-element.44), channel_id=1, source_target_pairs={{0,1},{1,0},{2,3},{3,2},{4,5},{5,4},{6,7},{7,6},{8,9},{9,8},{10,11... | collective-permute-start | bytes 196616 | tf_op jit(solution)/shard_map/ppermute | solution.py:353
